TPU v7x, 128 devices: a whole 4x4x4 slice. The times are simulated.
128 devices in a mesh: clu: 32 (over z, x, core), frq: 4 (over y).
Axes of the slice: x: 4, y: 4, z: 4, core: 2. Of those that a mesh axis runs over, the one named last changes fastest.
Arguments:
- incident: float32 [4, 2, 65536, 128], P('frq', None, 'clu'), may hold values from -6 to 6
- initial: float32 [4, 2, 65536, 128], P('frq', None, 'clu'), may hold values from -3 to 3
- near_blocks: bfloat16 [512, 8, 4, 2, 128, 128], P('clu', None, 'frq'), may hold values from -0.125 to 0.125
- near_pattern: int32 [512, 8], P('clu'), may hold values from 0 to 47
- crack_blocks: bfloat16 [1024, 4, 2, 128, 128], P('clu', 'frq'), may hold values from -0.25 to 0.25
- crack_cluster: int32 [1024, 1], P('clu'), may hold values from 0 to 31; in each aligned block of 32 rows (0 to 31, 32 to 63, ...) at most 2 rows name the same one
- crack_source: int32 [1024], P('clu'), may hold values from 0 to 3
- crack_target: int32 [1024], P('clu'), may hold values from 0 to 15
- pulse_spectrum: float32 [4, 2], P('frq'), may hold values from -4 to 4
Outputs:
- scattered: float32 [4, 2, 65536, 128], P('frq', None, 'clu')
- time_trace: float32 [4, 65536, 128], P('frq', 'clu')
Inputs may be any that keep to these rules, and one draw needn't show every extreme that they name: `crack_cluster`: in the rows of one cluster no source cluster is named more than 2 times, a bound that some block reaches.
All inputs are finite; a program needn't handle non-finite values.
Results may differ from a plain program's by a relative error of at most 0.0014.
Values may be sent and summed in bfloat16 or wider, within the bound.
A program may use at most 128 MiB of HBM per device.

v0:
```python
import jax
import jax.numpy as jnp
from jax import lax
from jax.sharding import PartitionSpec as P

FR_DEV = 1


epsilon = 1e-06


def with_halo(block, sides, width):
    for axis, dim in sides:
        count = lax.axis_size(axis)
        forward = [(i, i + 1) for i in range(count - 1)]
        forward.append((count - 1, 0))
        backward = [(target, source) for source, target in forward]
        low = lax.ppermute(
            lax.slice_in_dim(block, block.shape[dim] - width, None, axis=dim), axis, forward
        )
        high = lax.ppermute(lax.slice_in_dim(block, 0, width, axis=dim), axis, backward)
        block = jnp.concatenate([low, block, high], axis=dim)
    return block


def complex_times(factor, vector):
    real_part = factor[0][:, None, :] * vector[:, 0] - factor[1][:, None, :] * vector[:, 1]
    imag_part = factor[0][:, None, :] * vector[:, 1] + factor[1][:, None, :] * vector[:, 0]
    return jnp.stack([real_part, imag_part], axis=1)


def inner_local(former, latter):
    real_part = jnp.sum(former[:, 0] * latter[:, 0] + former[:, 1] * latter[:, 1], axis=1)
    imag_part = jnp.sum(former[:, 0] * latter[:, 1] - former[:, 1] * latter[:, 0], axis=1)
    return (real_part, imag_part)


def square_local(vector):
    return jnp.sum(vector[:, 0] * vector[:, 0] + vector[:, 1] * vector[:, 1], axis=1)


def least_squares(beta_norm, first_h, sub_one, second_h, third_h, sub_two):
    r_one = jnp.sqrt(first_h[0] ** 2 + first_h[1] ** 2 + sub_one**2)
    q_real = first_h[0] / r_one
    q_imag = first_h[1] / r_one
    q_low = sub_one / r_one
    mix_real = q_real * second_h[0] + q_imag * second_h[1] + q_low * third_h[0]
    mix_imag = q_real * second_h[1] - q_imag * second_h[0] + q_low * third_h[1]
    top_real = second_h[0] - (mix_real * q_real - mix_imag * q_imag)
    top_imag = second_h[1] - (mix_real * q_imag + mix_imag * q_real)
    mid_real = third_h[0] - mix_real * q_low
    mid_imag = third_h[1] - mix_imag * q_low
    r_two_sq = top_real**2 + top_imag**2 + mid_real**2 + mid_imag**2 + sub_two**2
    later_real = beta_norm * top_real / r_two_sq
    later_imag = -beta_norm * top_imag / r_two_sq
    early_real = (beta_norm * q_real - (mix_real * later_real - mix_imag * later_imag)) / r_one
    early_imag = (-beta_norm * q_imag - (mix_real * later_imag + mix_imag * later_real)) / r_one
    return ((early_real, early_imag), (later_real, later_imag))


def project(vectors, latter):
    terms = []
    for former in vectors:
        real_part, imag_part = inner_local(former, latter)
        terms.append(real_part)
        terms.append(imag_part)
    summed = lax.psum(tuple(terms), "clu")
    return [(summed[2 * place], summed[2 * place + 1]) for place in range(len(vectors))]


def lengths(vector):
    return lax.psum(square_local(vector), "clu")


def arnoldi_column(vectors, image):
    heights = project(vectors, image)
    for height, former in zip(heights, vectors):
        image = image - complex_times(height, former)
    squared = lengths(image)
    return (heights, image, jnp.sqrt(squared + epsilon))


def local(
    incident,
    initial,
    near_blocks,
    near_pattern,
    crack_blocks,
    crack_cluster,
    crack_source,
    crack_target,
    pulse_spectrum,
):
    freq_dev = incident.shape[0]
    panels = incident.shape[2]
    directions = incident.shape[3]
    nblocks = near_blocks.shape[0]
    near_span = near_blocks.shape[1]
    block_width = near_blocks.shape[4]
    edges = crack_blocks.shape[0]
    clusters = lax.axis_size("clu")
    capacity = max(2, (2 * edges + clusters - 1) // clusters)
    near_flat = near_pattern.reshape(-1)
    source_cluster = crack_cluster[:, 0]
    target_hot = (crack_target[None, :] == jnp.arange(nblocks, dtype=jnp.int32)[:, None]).astype(
        jnp.float32
    )
    edge_ids = jnp.arange(edges, dtype=jnp.int32)
    same_source = source_cluster[:, None] == source_cluster[None, :]
    earlier = edge_ids[:, None] > edge_ids[None, :]
    slot_rank = jnp.sum((same_source & earlier).astype(jnp.int32), axis=1)
    slot_index = source_cluster * capacity + slot_rank
    slot_hot = (
        slot_index[:, None] == jnp.arange(clusters * capacity, dtype=jnp.int32)[None, :]
    ).astype(jnp.int32)
    wanted = jnp.sum(slot_hot * crack_source[:, None], axis=0)
    requested = lax.all_to_all(wanted, "clu", split_axis=0, concat_axis=0, tiled=True)

    def fetch(vec_low):
        picked = jnp.take(vec_low, requested, axis=2)
        received = lax.all_to_all(picked, "clu", split_axis=2, concat_axis=2, tiled=True)
        return jnp.take(received, slot_index, axis=2)

    def apply(vector):
        vec_low = vector.astype(jnp.bfloat16).reshape(freq_dev, 2, nblocks, block_width, directions)
        extended = with_halo(vec_low, (("clu", 2),), nblocks)
        columns = jnp.take(extended, near_flat, axis=2).reshape(
            freq_dev, 2, nblocks, near_span, block_width, directions
        )
        products = jnp.einsum(
            "bsfcpq,fdbsqk->fcdbpk", near_blocks, columns, preferred_element_type=jnp.float32
        )
        near_real = products[:, 0, 0] - products[:, 1, 1]
        near_imag = products[:, 0, 1] + products[:, 1, 0]
        chosen = fetch(vec_low)
        crack_prod = jnp.einsum(
            "efcpq,fdeqk->fcdepk", crack_blocks, chosen, preferred_element_type=jnp.float32
        )
        crack_real = crack_prod[:, 0, 0] - crack_prod[:, 1, 1]
        crack_imag = crack_prod[:, 0, 1] + crack_prod[:, 1, 0]
        added_real = jnp.einsum(
            "be,fepk->fbpk", target_hot, crack_real, precision=lax.Precision.HIGHEST
        )
        added_imag = jnp.einsum(
            "be,fepk->fbpk", target_hot, crack_imag, precision=lax.Precision.HIGHEST
        )
        result = jnp.stack([near_real + added_real, near_imag + added_imag], axis=1)
        return 0.5 * vector + result.reshape(freq_dev, 2, panels, directions)

    residual = incident - apply(initial)
    beta_norm = jnp.sqrt(lax.psum(square_local(residual), "clu") + epsilon)
    basis_one = residual / beta_norm[:, None, None, :]
    heights, image, sub_one = arnoldi_column([basis_one], apply(basis_one))
    first_h = heights[0]
    basis_two = image / sub_one[:, None, None, :]
    heights, image, sub_two = arnoldi_column([basis_one, basis_two], apply(basis_two))
    early, later = least_squares(beta_norm, first_h, sub_one, heights[0], heights[1], sub_two)
    scattered = initial + complex_times(early, basis_one) + complex_times(later, basis_two)
    total_times = FR_DEV * lax.axis_size("frq")
    times = jnp.arange(FR_DEV * lax.axis_size("frq"), dtype=jnp.int32).astype(jnp.float32)[:, None]
    freqs = (lax.axis_index("frq") * freq_dev + jnp.arange(freq_dev, dtype=jnp.int32)).astype(
        jnp.float32
    )[None, :]
    angle = 2.0 * jnp.pi * times * freqs / total_times
    coef_real = pulse_spectrum[None, :, 0] * jnp.cos(angle) - pulse_spectrum[None, :, 1] * jnp.sin(
        angle
    )
    coef_imag = -(
        pulse_spectrum[None, :, 0] * jnp.sin(angle) + pulse_spectrum[None, :, 1] * jnp.cos(angle)
    )
    term = jnp.einsum("tf,fpk->tpk", coef_real, scattered[:, 0], precision=lax.Precision.HIGHEST)
    time_trace = lax.psum_scatter(
        term
        + jnp.einsum("tf,fpk->tpk", coef_imag, scattered[:, 1], precision=lax.Precision.HIGHEST),
        "frq",
        scatter_dimension=0,
        tiled=True,
    )
    return (scattered, time_trace)


def solution(mesh):
    in_specs = (
        P("frq", None, "clu", None),
        P("frq", None, "clu", None),
        P("clu", None, "frq", None, None, None),
        P("clu", None),
        P("clu", "frq", None, None, None),
        P("clu", None),
        P("clu"),
        P("clu"),
        P("frq", None),
    )
    out_specs = (P("frq", None, "clu", None), P("frq", "clu", None))
    return jax.shard_map(local, mesh=mesh, in_specs=in_specs, out_specs=out_specs, check_vma=False)
```

profile of v0, /device:TPU:1, one launch (start us, length us, event | category | flops | bytes accessed | tf_op | source)
XLA Modules:
  0.0 826.6 jit_solution(18087410245463403512)
XLA Ops:
  10.3 9.4 %all-to-all-start = ((s32[32,2,1]{1,2,0:T(1,128)}), s32[32,2,1]{1,2,0:T(1,128)S(1)}, u32[]{:S(2)}, u32[]{:S(2)}) async-start(s32[32,2,1]{1,2,0:T(1,128)} %bitcast.17), calls=%async_computation | async-start | bytes 32768 | tf_op jit(solution)/shard_map/all_to_all | solution.py:117
  21.5 5.2 all-to-all-done
  31.0 4.6 fusion.11
  35.6 5.2 all-to-all-start.1
  42.8 56.9 %collective-permute-done = bf16[1,2,16,128,128]{4,3,2,1,0:T(8,128)(2,1)} collective-permute-done((bf16[1,2,16,128,128]{4,3,2,1,0:T(8,128)(2,1)S(1)}, bf16[1,2,16,128,128]{4,3,2,1,0:T(8,128)(2,1)}, u32[]{:S(2)}, u32[]{:S(2)}) %collective-permute-start) | collective-permute-done | bytes 1048608 | tf_op jit(solution)/shard_map/ppermute | solution.py:18
  102.0 3.5 maximum_bitcast_fusion
  105.5 8.5 %gather_fusion = bf16[128,2,128,128]{3,2,1,0:T(8,128)(2,1)} fusion(bf16[2,48,128,128]{3,2,1,0:T(8,128)(2,1)} %maximum_bitcast_fusion, s32[1024]{0:T(1024)S(1)} %pad_clamp_fusion.2), kind=kCustom, calls=%fused_computation.clone | custom fusion | bytes 16777728 | tf_op jit(solution)/shard_map/jit(_take)/gather | solution.py:127
  114.0 7.4 bitcast_select_fusion.2
  121.4 10.0 %fusion.12 = f32[1,2,2,16,128,128]{5,4,1,2,3,0:T(8,128)} fusion(bf16[2,16,8,128,128,1]{4,3,0,2,1,5:T(8,128)(2,1)} %bitcast.313, bf16[16,8,1,2,128,128]{5,4,3,2,1,0:T(8,128)(2,1)} %param.17), kind=kOutput, calls=%fused_computation.37 | convolution fusion | flops 2147483648 | bytes 20971520 | tf_op jit(solution)/shard_map/bsfcpq,fdbsqk->fcdbpk/dot_general | solution.py:130
  131.4 4.7 copy.213
  136.2 4.3 gather_fusion.2
  140.5 3.7 convolution_bitcast_fusion.2
  146.9 3.1 copy.119
  150.0 3.1 copy.117
  160.7 64.2 %psum.75 = f32[1,128]{1,0:T(1,128)S(1)} all-reduce(f32[1,128]{1,0:T(1,128)S(1)} %bitcast.333), channel_id=1, replica_groups=mesh['clu'=32,'frq'=4] {'clu'}, use_global_device_ids=true, to_apply=%region_3.0 | all-reduce | flops 128 | bytes 1024 | tf_op jit(solution)/shard_map/psum | solution.py:151
  224.9 3.2 fusion.98
  231.2 4.6 fusion.10
  235.7 6.3 all-to-all-start.2
  243.8 57.2 %collective-permute-done.2 = bf16[1,2,16,128,128]{4,3,2,1,0:T(8,128)(2,1)S(1)} collective-permute-done((bf16[1,2,16,128,128]{4,3,2,1,0:T(8,128)(2,1)S(1)}, bf16[1,2,16,128,128]{4,3,2,1,0:T(8,128)(2,1)S(1)}, u32[]{:S(2)}, u32[]{:S(2)}) %collective-permute-start.2) | collective-permute-done | bytes 1048608 | tf_op jit(solution)/shard_map/ppermute | solution.py:18
  305.1 8.5 %gather_fusion.3 = bf16[128,2,128,128]{3,2,1,0:T(8,128)(2,1)} fusion(bf16[2,48,128,128]{3,2,1,0:T(8,128)(2,1)} %maximum_bitcast_fusion.1, s32[1024]{0:T(1024)S(1)} %pad_clamp_fusion.2), kind=kCustom, calls=%fused_computation.3.clone | custom fusion | bytes 16777728 | tf_op jit(solution)/shard_map/jit(_take)/gather | solution.py:127
  313.5 7.4 bitcast_select_fusion.1
  320.9 10.1 %fusion.17 = f32[1,2,2,16,128,128]{5,4,1,2,3,0:T(8,128)} fusion(bf16[2,16,8,128,128,1]{4,3,0,2,1,5:T(8,128)(2,1)} %bitcast.314, bf16[16,8,1,2,128,128]{5,4,3,2,1,0:T(8,128)(2,1)} %param.17), kind=kOutput, calls=%fused_computation.38 | convolution fusion | flops 2147483648 | bytes 20971520 | tf_op jit(solution)/shard_map/bsfcpq,fdbsqk->fcdbpk/dot_general | solution.py:130
  331.0 4.7 copy.212
  335.7 4.3 gather_fusion.5
  340.1 3.7 convolution_bitcast_fusion.1
  346.4 3.1 copy.129
  349.6 3.4 fusion.72
  353.0 3.1 copy.127
  358.6 3.2 fusion.56
  363.1 64.3 %all-reduce.1 = (f32[1,128]{1,0:T(1,128)S(1)}, f32[1,128]{1,0:T(1,128)S(1)}) all-reduce(f32[1,128]{1,0:T(1,128)S(1)} %bitcast.330, f32[1,128]{1,0:T(1,128)S(1)} %bitcast.329), channel_id=1, replica_groups=mesh['clu'=32,'frq'=4] {'clu'}, use_global_device_ids=true, to_apply=%region_7.11 | all-reduce | flops 256 | bytes 2048 | tf_op jit(solution)/shard_map/psum | solution.py:67
  431.0 63.9 %psum.80 = f32[1,128]{1,0:T(1,128)S(1)} all-reduce(f32[1,128]{1,0:T(1,128)S(1)} %bitcast.331), channel_id=1, replica_groups=mesh['clu'=32,'frq'=4] {'clu'}, use_global_device_ids=true, to_apply=%region_9.13 | all-reduce | flops 128 | bytes 1024 | tf_op jit(solution)/shard_map/psum | solution.py:72
  494.9 4.6 fusion.97
  502.5 4.6 fusion.9
  507.1 5.2 all-to-all-start.3
  516.0 55.2 %collective-permute-done.4 = bf16[1,2,16,128,128]{4,3,2,1,0:T(8,128)(2,1)} collective-permute-done((bf16[1,2,16,128,128]{4,3,2,1,0:T(8,128)(2,1)S(1)}, bf16[1,2,16,128,128]{4,3,2,1,0:T(8,128)(2,1)}, u32[]{:S(2)}, u32[]{:S(2)}) %collective-permute-start.4) | collective-permute-done | bytes 1048608 | tf_op jit(solution)/shard_map/ppermute | solution.py:18
  576.5 8.5 %gather_fusion.6 = bf16[128,2,128,128]{3,2,1,0:T(8,128)(2,1)} fusion(bf16[2,48,128,128]{3,2,1,0:T(8,128)(2,1)} %maximum_bitcast_fusion.2, s32[1024]{0:T(1024)S(1)} %pad_clamp_fusion.2), kind=kCustom, calls=%fused_computation.4.clone | custom fusion | bytes 16777728 | tf_op jit(solution)/shard_map/jit(_take)/gather | solution.py:127
  585.0 7.4 bitcast_select_fusion
  592.4 10.0 %fusion.22 = f32[1,2,2,16,128,128]{5,4,1,2,3,0:T(8,128)} fusion(bf16[2,16,8,128,128,1]{4,3,0,2,1,5:T(8,128)(2,1)} %bitcast.312, bf16[16,8,1,2,128,128]{5,4,3,2,1,0:T(8,128)(2,1)} %param.17), kind=kOutput, calls=%fused_computation.39 | convolution fusion | flops 2147483648 | bytes 20971520 | tf_op jit(solution)/shard_map/bsfcpq,fdbsqk->fcdbpk/dot_general | solution.py:130
  602.4 4.7 copy.211
  607.2 4.3 gather_fusion.8
  611.5 3.7 convolution_bitcast_fusion
  617.9 3.1 copy.139
  621.0 3.4 fusion.68
  624.4 3.3 copy.137
  630.2 3.2 fusion.50
  636.2 64.1 %all-reduce = (f32[1,128]{1,0:T(1,128)S(1)}, f32[1,128]{1,0:T(1,128)S(1)}, f32[1,128]{1,0:T(1,128)S(1)}, f32[1,128]{1,0:T(1,128)S(1)}) all-reduce(f32[1,128]{1,0:T(1,128)S(1)} %bitcast.326, f32[1,128]{1,0:T(1,128)S(1)} %bitcast.327, f32[1,128]{1,0:T(1,128)S(1)} %bitcast.328, ...), channel_id=1, replica_groups=mesh['clu'=32,'frq'=4] {'clu'}, use_global_device_ids=true, to_apply=%region_17.21 | all-reduce | flops 512 | bytes 4096 | tf_op jit(solution)/shard_map/psum | solution.py:67
  704.0 63.9 %psum.89 = f32[1,128]{1,0:T(1,128)S(1)} all-reduce(f32[1,128]{1,0:T(1,128)S(1)} %bitcast.332), channel_id=1, replica_groups=mesh['clu'=32,'frq'=4] {'clu'}, use_global_device_ids=true, to_apply=%region_19.23 | all-reduce | flops 128 | bytes 1024 | tf_op jit(solution)/shard_map/psum | solution.py:72
  775.9 43.3 %reduce-scatter.2.cloned.1.call-done = f32[1,2048,128]{2,1,0:T(8,128)} async-done(((f32[4,2048,128]{2,1,0:T(8,128)}), f32[1,2048,128]{2,1,0:T(8,128)}) %reduce-scatter.2.cloned.1.call-update) | async-done | bytes 1048592 | tf_op jit(solution)/shard_map/reduce_scatter | solution.py:172
  (123 shorter events, 74.3 us)
Async XLA Ops:
  7.2 133.3 %copy-start = (bf16[32,1,2,128,128]{4,3,2,1,0:T(8,128)(2,1)S(1)}, bf16[32,1,2,128,128]{4,3,2,1,0:T(8,128)(2,1)}, u32[]{:S(2)}) copy-start(bf16[32,1,2,128,128]{4,3,2,1,0:T(8,128)(2,1)} %param.19) | copy-start | bytes 6291460
  10.3 16.3 %all-to-all-start = ((s32[32,2,1]{1,2,0:T(1,128)}), s32[32,2,1]{1,2,0:T(1,128)S(1)}, u32[]{:S(2)}, u32[]{:S(2)}) async-start(s32[32,2,1]{1,2,0:T(1,128)} %bitcast.17), calls=%async_computation | async-start | bytes 32768 | tf_op jit(solution)/shard_map/all_to_all | solution.py:117
  35.6 7.0 copy-start.24
  35.6 7.1 copy-start.26
  35.6 95.9 %all-to-all-start.1 = ((bf16[1,2,64,128,128]{4,3,1,0,2:T(8,128)(2,1)}), bf16[1,2,64,128,128]{4,3,1,0,2:T(8,128)(2,1)}, u32[]{:S(2)}, u32[]{:S(2)}) async-start(bf16[1,2,64,128,128]{4,3,1,0,2:T(8,128)(2,1)} %fusion.11), calls=%async_computation.1 | async-start | bytes 8388608 | tf_op jit(solution)/shard_map/all_to_all | solution.py:121
  40.8 58.9 %collective-permute-start = (bf16[1,2,16,128,128]{4,3,2,1,0:T(8,128)(2,1)S(1)}, bf16[1,2,16,128,128]{4,3,2,1,0:T(8,128)(2,1)}, u32[]{:S(2)}, u32[]{:S(2)}) collective-permute-start(bf16[1,2,16,128,128]{4,3,2,1,0:T(8,128)(2,1)S(1)} %bitcast.292), channel_id=1, source_target_pairs={{0,4},{4,8},{8,12},{12,16},{16,20},{20,24},{24,28},{28,32},{32,36}... | collective-permute-start | bytes 3145736 | tf_op jit(solution)/shard_map/ppermute | solution.py:18
  42.5 59.5 %collective-permute-start.1 = (bf16[1,2,16,128,128]{4,3,2,1,0:T(8,128)(2,1)S(1)}, bf16[1,2,16,128,128]{4,3,2,1,0:T(8,128)(2,1)}, u32[]{:S(2)}, u32[]{:S(2)}) collective-permute-start(bf16[1,2,16,128,128]{4,3,2,1,0:T(8,128)(2,1)S(1)} %bitcast.293), channel_id=1, source_target_pairs={{4,0},{8,4},{12,8},{16,12},{20,16},{24,20},{28,24},{32,28},{36,32}... | collective-permute-start | bytes 3145736 | tf_op jit(solution)/shard_map/ppermute | solution.py:21
  150.0 3.1 copy-start.23
  153.1 2.6 copy-start.17
  153.1 3.5 copy-start.19
  156.6 1.6 copy-start.8
  156.6 2.2 copy-start.22
  159.1 1.3 copy-start.7
  235.7 95.3 %all-to-all-start.2 = ((bf16[1,2,64,128,128]{4,3,1,0,2:T(8,128)(2,1)}), bf16[1,2,64,128,128]{4,3,1,0,2:T(8,128)(2,1)}, u32[]{:S(2)}, u32[]{:S(2)}) async-start(bf16[1,2,64,128,128]{4,3,1,0,2:T(8,128)(2,1)} %fusion.10), calls=%async_computation.2 | async-start | bytes 8388608 | tf_op jit(solution)/shard_map/all_to_all | solution.py:121
  242.1 58.9 %collective-permute-start.2 = (bf16[1,2,16,128,128]{4,3,2,1,0:T(8,128)(2,1)S(1)}, bf16[1,2,16,128,128]{4,3,2,1,0:T(8,128)(2,1)S(1)}, u32[]{:S(2)}, u32[]{:S(2)}) collective-permute-start(bf16[1,2,16,128,128]{4,3,2,1,0:T(8,128)(2,1)S(1)} %bitcast.296), channel_id=1, source_target_pairs={{0,4},{4,8},{8,12},{12,16},{16,20},{20,24},{24,28},{28,32},{32,36}... | collective-permute-start | bytes 3145736 | tf_op jit(solution)/shard_map/ppermute | solution.py:18
  243.8 59.4 %collective-permute-start.3 = (bf16[1,2,16,128,128]{4,3,2,1,0:T(8,128)(2,1)S(1)}, bf16[1,2,16,128,128]{4,3,2,1,0:T(8,128)(2,1)S(1)}, u32[]{:S(2)}, u32[]{:S(2)}) collective-permute-start(bf16[1,2,16,128,128]{4,3,2,1,0:T(8,128)(2,1)S(1)} %bitcast.297), channel_id=1, source_target_pairs={{4,0},{8,4},{12,8},{16,12},{20,16},{24,20},{28,24},{32,28},{36,32}... | collective-permute-start | bytes 3145736 | tf_op jit(solution)/shard_map/ppermute | solution.py:21
  356.0 2.5 copy-start.20
  358.5 3.3 copy-start.1
  361.8 1.0 copy-start.11
  361.8 67.5 %copy-start.10 = (f32[1,16,128,128]{3,2,1,0:T(8,128)}, f32[1,16,128,128]{3,2,1,0:T(8,128)S(1)}, u32[]{:S(2)}) copy-start(f32[1,16,128,128]{3,2,1,0:T(8,128)S(1)} %get-tuple-element.43) | copy-start | bytes 3145732
  427.4 2.2 copy-start.2
  427.4 2.5 copy-start.12
  429.3 1.0 copy-start.13
  429.3 1.4 copy-start.14
  507.1 7.0 copy-start.25
  507.1 95.4 %all-to-all-start.3 = ((bf16[1,2,64,128,128]{4,3,1,0,2:T(8,128)(2,1)}), bf16[1,2,64,128,128]{4,3,1,0,2:T(8,128)(2,1)}, u32[]{:S(2)}, u32[]{:S(2)}) async-start(bf16[1,2,64,128,128]{4,3,1,0,2:T(8,128)(2,1)} %fusion.9), calls=%async_computation.3 | async-start | bytes 8388608 | tf_op jit(solution)/shard_map/all_to_all | solution.py:121
  512.3 307.0 %reduce-scatter.2.cloned.1.call-start = ((), (), s32[]{:S(2)}) async-start(), calls=%async_computation.5 | async-start | bytes 5242880 | tf_op jit(solution)/shard_map/reduce_scatter | solution.py:172
  512.4 58.8 %collective-permute-start.4 = (bf16[1,2,16,128,128]{4,3,2,1,0:T(8,128)(2,1)S(1)}, bf16[1,2,16,128,128]{4,3,2,1,0:T(8,128)(2,1)}, u32[]{:S(2)}, u32[]{:S(2)}) collective-permute-start(bf16[1,2,16,128,128]{4,3,2,1,0:T(8,128)(2,1)S(1)} %bitcast.288), channel_id=1, source_target_pairs={{0,4},{4,8},{8,12},{12,16},{16,20},{20,24},{24,28},{28,32},{32,36}... | collective-permute-start | bytes 3145736 | tf_op jit(solution)/shard_map/ppermute | solution.py:18
  514.1 59.5 %collective-permute-start.5 = (bf16[1,2,16,128,128]{4,3,2,1,0:T(8,128)(2,1)S(1)}, bf16[1,2,16,128,128]{4,3,2,1,0:T(8,128)(2,1)}, u32[]{:S(2)}, u32[]{:S(2)}) collective-permute-start(bf16[1,2,16,128,128]{4,3,2,1,0:T(8,128)(2,1)S(1)} %bitcast.289), channel_id=1, source_target_pairs={{4,0},{8,4},{12,8},{16,12},{20,16},{24,20},{28,24},{32,28},{36,32}... | collective-permute-start | bytes 3145736 | tf_op jit(solution)/shard_map/ppermute | solution.py:21
  627.7 2.5 copy-start.21
  630.2 3.3 copy-start.5
  633.4 1.0 copy-start.15
  633.5 2.0 copy-start.3
  700.3 2.9 copy-start.6
  700.3 3.1 copy-start.16
  768.0 2.2 copy-start.4
  770.3 1.6 copy-start.9
  772.2 1.3 copy-start.18
Sparse Core Ops, SparseCore 0:
  776.1 43.1 reduce-scatter.1
where the time goes:
time: 831 us; the launch traced here: 827 us
  blocking collectives  320 us (39%)
  waiting for transfers between devices  225 us (27%)
  local copies, waits for them, and re-layouts  92.1 us (11%)
  other arithmetic  86.8 us (10%)
  matrix products  56.2 us (7%)
  starting transfers between devices  31.4 us (4%)
  between operations  14.9 us (2%)
    ppermute x3, waiting for transfers between devices, with_halo(): lax.ppermute(lax.slice_in_dim(block, block.shape[dim] - width, None, axis...  169 us
    psum x2, blocking collectives, project(): summed = lax.psum(tuple(terms), 'clu')  128 us
    psum x2, blocking collectives, lengths(): return lax.psum(square_local(vector), 'clu')  128 us
    psum x1, blocking collectives, local(): beta_norm = jnp.sqrt(lax.psum(square_local(residual), 'clu') + epsilon)  64.2 us
    reduce_scatter x1, waiting for transfers between devices, local(): lax.psum_scatter(term + jnp.einsum('tf,fpk->tpk', coef_imag, scattered[:,...  43.3 us
    dot_general x3, matrix products, apply(): jnp.einsum('bsfcpq,fdbsqk->fcdbpk', near_blocks, columns, preferred_eleme...  30.1 us
    gather x3, local copies, waits for them, and re-layouts, apply(): jnp.take(extended, near_flat, axis=2)  25.4 us
    select_n x4, other arithmetic, apply(): jnp.take(extended, near_flat, axis=2)  22.3 us
  transfers between devices with their start and end apart: 11, of which 8 were waited for; matrix products, arithmetic and copies ran while one was open for 11% of the time, Pallas kernels for 0%

commit v1 on v0

v1 whole, which is shorter than its diff:
```python
import functools

import jax
import jax.numpy as jnp
from jax import lax
from jax.experimental import pallas as pl
from jax.experimental.pallas import tpu as pltpu
from jax.sharding import PartitionSpec as P

MESH = pl.DeviceIdType.MESH
F32, BF16, I32 = jnp.float32, jnp.bfloat16, jnp.int32
EPS = 1e-06
BLK = 128
NB = 16
NEAR = 8
EDGES = 32
HALF = BLK // 2
SET = 8
PANELS = NB * BLK
NX = NZ = NY = 4
SPLIT = 6


def add4(a, d):
    return lax.rem(a + (d % 4), 4)


def kernel(
    pat, ccl, csrc, links, pulse, inc_hbm, ini_hbm, near_hbm, crack_hbm,
    scat_hbm, trace_hbm,
    A, C, R, X0, W, Y, prod, xe0, xe1, ag0, ag1,
    part2, sendp, sendm, half_in, full_in, far_r, far_w,
    rowbuf, colbuf, gbuf,
    load_sem, out_sem, ag_recv, ag_send, pair_recv, halo_recv, halo_send,
    y_recv, y_send, row_recv, row_send, col_recv, col_send, g_recv, g_send,
):
    me, yy = lax.axis_index("clu"), lax.axis_index("frq")
    core, xx = lax.rem(me, 2), lax.rem(lax.div(me, 2), 4)
    zz = lax.div(me, 8)
    spot = lax.rem(me, 8)

    def clu(dx, dz):
        return (add4(zz, dz) * 4 + add4(xx, dx)) * 2 + core

    partner = me + 1 - 2 * core
    right, left = lax.rem(me + 1, 32), lax.rem(me + 31, 32)

    def dev(c):
        return (c, yy)

    def ydev(dy):
        return (me, add4(yy, dy))

    def row_peer(i):
        return (me - spot + lax.rem(spot + i, 8), yy)

    def copy(src, dst, ssem, rsem, target):
        return pltpu.make_async_remote_copy(
            src_ref=src, dst_ref=dst, send_sem=ssem, recv_sem=rsem,
            device_id=target, device_id_type=MESH)

    def arrived(ref, ssem, rsem, source):
        copy(ref, ref, ssem, rsem, source).wait_recv()

    loads = [
        pltpu.make_async_copy(s, d, load_sem.at[i])
        for i, (s, d) in enumerate([(ini_hbm, X0), (near_hbm, A), (inc_hbm, R), (crack_hbm, C)])
    ]
    for l in loads:
        l.start()
    barrier = pltpu.get_barrier_semaphore()
    peers = [row_peer(i) for i in range(1, 8)]
    peers += [dev(clu(0, d)) for d in (1, 2, 3)]
    peers += [ydev(d) for d in (1, 2, 3)]
    peers += [dev(right), dev(left)]
    for p in peers:
        pl.semaphore_signal(barrier, inc=1, device_id=p, device_id_type=MESH)

    def rows_of(g):
        return pl.ds(pl.multiple_of(g * BLK, BLK), BLK)

    def put_low(re, im, g, xe, ag):
        low = jnp.concatenate([re.astype(BF16), im.astype(BF16)], axis=1)
        xe[NB + g] = low
        if ag is not None:
            ag[pl.ds(me * SET + 2 * g, 2)] = low.reshape(2, HALF, 2 * BLK)

    def gather_steps(parity, ag, group, off, n, x_first):
        hn = n // 2
        base = 22 * group

        def at(dp, ds):
            return clu(dp, ds) if x_first else clu(ds, dp)

        def region(c, part):
            start, length = {0: (off, n), 1: (off, hn), 2: (off + hn, hn)}[part]
            return ag.at[pl.ds(c * SET + start, length)]

        def send(c, part, target, slot):
            r = region(c, part)
            copy(r, r, ag_send.at[parity], ag_recv.at[parity, base + slot], dev(target)).start()

        def wait(c, part, source, slot):
            arrived(region(c, part), ag_send.at[parity], ag_recv.at[parity, base + slot], dev(source))

        def share(c, part):
            r = region(c, part)
            copy(r, r, ag_send.at[parity], pair_recv.at[parity], dev(partner)).start()

        cols = [0, -1, 1]

        def first():
            send(me, 0, at(1, 0), 0)
            send(me, 0, at(-1, 0), 1)
            send(me, 0, at(0, 1), 4)
            send(me, 0, at(0, -1), 5)
            share(me, 0)

        def primary(sign):
            def step():
                c = at(-sign, 0)
                wait(c, 0, c, 0 if sign > 0 else 1)
                send(c, 1 if sign > 0 else 2, at(sign, 0), 2 if sign > 0 else 3)
                k = 1 if sign > 0 else 2
                send(c, 0, at(0, 1), 4 + 4 * k)
                send(c, 0, at(0, -1), 5 + 4 * k)
                share(c, 0)
            return step

        def far(sign):
            def step():
                c, part = at(2, 0), 1 if sign > 0 else 2
                wait(c, part, at(-sign, 0), 2 if sign > 0 else 3)
                slot = 16 if sign > 0 else 18
                send(c, part, at(0, 1), slot)
                send(c, part, at(0, -1), slot + 1)
                share(c, part)
            return step

        def second(k, sign):
            def step():
                c = at(cols[k], -sign)
                wait(c, 0, at(0, -sign), 4 + 4 * k + (0 if sign > 0 else 1))
                send(c, 1 if sign > 0 else 2, at(0, sign), 6 + 4 * k + (0 if sign > 0 else 1))
                share(c, 0)
            return step

        def second_far(part, sign):
            def step():
                c = at(2, -sign)
                slot = 16 if part == 1 else 18
                wait(c, part, at(0, -sign), slot + (0 if sign > 0 else 1))
                if (part == 1) == (sign > 0):
                    send(c, part, at(0, sign), 20 if sign > 0 else 21)
                share(c, part)
            return step

        def final(k, sign):
            def step():
                c, part = at(2 if k == 3 else cols[k], 2), 1 if sign > 0 else 2
                slot = (20 if k == 3 else 6 + 4 * k) + (0 if sign > 0 else 1)
                wait(c, part, at(0, -sign), slot)
                share(c, part)
            return step

        early = [primary(1), primary(-1)]
        early += [second(0, 1), second(0, -1)]
        middle = [second(1, 1), second(1, -1), second(2, 1), second(2, -1), far(1), far(-1)]
        late = [second_far(1, 1), second_far(2, -1), second_far(1, -1), second_far(2, 1)]
        late += [final(k, s) for k in range(4) for s in (1, -1)]
        return first, early, middle, late

    def gather(parity, ag):
        groups = [(0, SPLIT, True), (SPLIT, SET - SPLIT, False)]
        made = [gather_steps(parity, ag, i, *g) for i, g in enumerate(groups) if g[1]]
        firsts = [m[0] for m in made]
        mixed = [[s for steps in zip(*[m[k] for m in made]) for s in steps] for k in (1, 2, 3)]
        total = 0
        for _, n, _ in groups:
            total += 15 * n + 16 * n

        def finish():
            arrived(ag.at[pl.ds(0, 16 * SET)], ag_send.at[parity], pair_recv.at[parity], dev(partner))

        def drain():
            r = ag.at[pl.ds(0, total)]
            copy(r, r, ag_send.at[parity], pair_recv.at[parity], dev(partner)).wait_send()

        return firsts, mixed, finish, drain

    def halo_start(parity, xe):
        own = xe.at[pl.ds(NB, NB)]
        copy(own, xe.at[pl.ds(0, NB)], halo_send.at[parity], halo_recv.at[parity, 0], dev(right)).start()
        copy(own, xe.at[pl.ds(2 * NB, NB)], halo_send.at[parity], halo_recv.at[parity, 1], dev(left)).start()

    def halo_wait(parity, xe):
        arrived(xe.at[pl.ds(0, NB)], halo_send.at[parity], halo_recv.at[parity, 0], dev(left))
        arrived(xe.at[pl.ds(2 * NB, NB)], halo_send.at[parity], halo_recv.at[parity, 1], dev(right))

    def halo_drain(parity, xe):
        r = xe.at[pl.ds(0, 2 * NB)]
        copy(r, r, halo_send.at[parity], halo_recv.at[parity, 0], dev(right)).wait_send()

    def near_products(xe, steps):
        places = {}
        for i, s in enumerate(steps):
            places.setdefault(i * NB // len(steps), []).append(s)

        def row(g, carry):
            for k, todo in places.items():
                @pl.when(g == k)
                def _(todo=todo):
                    for s in todo:
                        s()
            acc = None
            for p in range(NEAR // 2):
                xs = jnp.concatenate([xe[pat[g, 2 * p]], xe[pat[g, 2 * p + 1]]], axis=0)
                ms = jnp.concatenate([A[g * NEAR + 2 * p], A[g * NEAR + 2 * p + 1]], axis=1)
                d = jnp.dot(ms, xs, preferred_element_type=F32)
                acc = d if acc is None else acc + d
            r = rows_of(g)
            Y[0, r, :] = acc[:BLK, :BLK] - acc[BLK:, BLK:]
            Y[1, r, :] = acc[:BLK, BLK:] + acc[BLK:, :BLK]
            return carry

        lax.fori_loop(0, NB, row, 0)

    def crack_products(ag):
        def edge(e, carry):
            q = ccl[e, 0] * 4 + csrc[e]
            xc = jnp.concatenate([ag[2 * q], ag[2 * q + 1]], axis=0)
            turned = jnp.concatenate([-xc[:, BLK:], xc[:, :BLK]], axis=1)
            xs = jnp.concatenate([xc, turned], axis=0)
            ms = jnp.concatenate([C[e, :BLK, :], C[e, BLK:, :]], axis=1)
            prod[e] = jnp.dot(ms, xs, preferred_element_type=F32) + prod[links[e]]
            return carry

        lax.fori_loop(0, EDGES, edge, 0)

    def total_of(g):
        r = rows_of(g)
        d = prod[links[EDGES + g]]
        return Y[0, r, :] + d[:, :BLK], Y[1, r, :] + d[:, BLK:]

    def fold(v):
        return jnp.sum(v.reshape(BLK // 8, 8, BLK), axis=0)

    zero8 = jnp.zeros((8, BLK), F32)

    def line(v):
        return jnp.sum(v, axis=0, keepdims=True)

    def clu_sum(k, lines):
        pad = [jnp.zeros((1, BLK), F32)] * (8 - len(lines))
        rowbuf[k, spot] = jnp.concatenate(lines + pad, axis=0)
        for i in range(1, 8):
            copy(rowbuf.at[k, spot], rowbuf.at[k, spot], row_send.at[k], row_recv.at[k], row_peer(i)).start()
        seven = rowbuf.at[k, pl.ds(0, 7)]
        copy(seven, seven, row_send.at[k], row_recv.at[k], row_peer(1)).wait()
        s = rowbuf[k, 0]
        for i in range(1, 8):
            s = s + rowbuf[k, i]
        colbuf[k, zz] = s
        for d in (1, 2, 3):
            copy(colbuf.at[k, zz], colbuf.at[k, zz], col_send.at[k], col_recv.at[k], dev(clu(0, d))).start()
        three = colbuf.at[k, pl.ds(0, 3)]
        copy(three, three, col_send.at[k], col_recv.at[k], dev(clu(0, 1))).wait()
        s = (colbuf[k, 0] + colbuf[k, 1]) + (colbuf[k, 2] + colbuf[k, 3])
        return [s[i:i + 1, :] for i in range(len(lines))]

    def far_steps(k, xe, dest):
        own = xe.at[pl.ds(NB, NB)]

        def first():
            copy(own, dest.at[0], y_send.at[k], y_recv.at[k, 0], ydev(1)).start()
            copy(own, dest.at[1], y_send.at[k], y_recv.at[k, 1], ydev(-1)).start()

        def up():
            arrived(dest.at[0], y_send.at[k], y_recv.at[k, 0], ydev(-1))
            copy(dest.at[0, pl.ds(0, NB // 2)], dest.at[2, pl.ds(0, NB // 2)],
                 y_send.at[k], y_recv.at[k, 2], ydev(1)).start()

        def down():
            arrived(dest.at[1], y_send.at[k], y_recv.at[k, 1], ydev(1))
            copy(dest.at[1, pl.ds(NB // 2, NB // 2)], dest.at[2, pl.ds(NB // 2, NB // 2)],
                 y_send.at[k], y_recv.at[k, 3], ydev(-1)).start()

        def done():
            arrived(dest.at[2, pl.ds(0, NB // 2)], y_send.at[k], y_recv.at[k, 2], ydev(-1))
            arrived(dest.at[2, pl.ds(NB // 2, NB // 2)], y_send.at[k], y_recv.at[k, 3], ydev(1))
            for i in (0, 1):
                pass
            r = dest.at[pl.ds(0, 3)]
            copy(r, r, y_send.at[k], y_recv.at[k, 0], ydev(1)).wait_send()

        return first, up, down, done

    def coef(t, f, pr, pi):
        m = lax.rem(t * f, 4)
        cs = jnp.where(m == 0, 1.0, jnp.where(m == 2, -1.0, 0.0)).astype(F32)
        sn = jnp.where(m == 1, 1.0, jnp.where(m == 3, -1.0, 0.0)).astype(F32)
        return pr * cs - pi * sn, -(pr * sn + pi * cs)

    own_pr, own_pi = pulse[0, 0], pulse[0, 1]
    MID = PANELS // 2

    def share_first():
        cr, ci = coef(add4(yy, 2), yy, own_pr, own_pi)

        def body(g, carry):
            r = rows_of(g)
            part2[r, :] = cr * X0[0, r, :] + ci * X0[1, r, :]
            return carry

        lax.fori_loop(0, NB, body, 0)
        lo, hi = part2.at[pl.ds(0, MID)], part2.at[pl.ds(MID, MID)]
        copy(lo, half_in.at[0], y_send.at[0], y_recv.at[0, 0], ydev(1)).start()
        copy(hi, half_in.at[1], y_send.at[0], y_recv.at[0, 1], ydev(-1)).start()

    def share_second():
        crp, cip = coef(add4(yy, 1), yy, own_pr, own_pi)
        crm, cim = coef(add4(yy, 3), yy, own_pr, own_pi)
        arrived(half_in.at[0], y_send.at[0], y_recv.at[0, 0], ydev(-1))
        arrived(half_in.at[1], y_send.at[0], y_recv.at[0, 1], ydev(1))

        def body(g, carry):
            r, q = rows_of(g), rows_of(g + NB // 2)
            a, b = X0[0, r, :], X0[1, r, :]
            sendp[r, :] = crp * a + cip * b + half_in[0, r, :]
            sendm[r, :] = crm * a + cim * b
            a, b = X0[0, q, :], X0[1, q, :]
            sendp[q, :] = crp * a + cip * b
            sendm[q, :] = crm * a + cim * b + half_in[1, r, :]
            return carry

        lax.fori_loop(0, NB // 2, body, 0)
        copy(sendp, full_in.at[0], y_send.at[3], y_recv.at[0, 2], ydev(1)).start()
        copy(sendm, full_in.at[1], y_send.at[3], y_recv.at[0, 3], ydev(-1)).start()

    def share_done():
        arrived(full_in.at[0], y_send.at[3], y_recv.at[0, 2], ydev(-1))
        arrived(full_in.at[1], y_send.at[3], y_recv.at[0, 3], ydev(1))
        copy(part2, part2, y_send.at[0], y_recv.at[0, 0], ydev(1)).wait_send()
        copy(full_in, full_in, y_send.at[3], y_recv.at[0, 0], ydev(1)).wait_send()

    def apply(parity, xe, ag, plan, y_steps):
        firsts, mixed, finish, drain = plan
        early, middle, late = mixed
        for s in early:
            s()
        for s in y_steps[:1]:
            s()
        for s in middle:
            s()
        halo_wait(parity, xe)
        near_products(xe, late + list(y_steps[1:]))
        finish()
        crack_products(ag)
        drain()
        halo_drain(parity, xe)

    loads[0].wait()

    def low_front(g, carry):
        r = rows_of(g)
        put_low(X0[0, r, :], X0[1, r, :], g, xe0, ag0)
        return carry

    def low_rest(g, carry):
        r = rows_of(g)
        put_low(X0[0, r, :], X0[1, r, :], g, xe0, None)
        return carry

    lax.fori_loop(0, 4, low_front, 0)
    pl.semaphore_wait(barrier, len(peers))
    plan = gather(0, ag0)
    for s in plan[0]:
        s()
    lax.fori_loop(4, NB, low_rest, 0)
    halo_start(0, xe0)
    share_first()

    prod[EDGES] = jnp.zeros((BLK, 2 * BLK), F32)
    loads[1].wait()
    loads[2].wait()
    loads[3].wait()

    apply(0, xe0, ag0, plan, (share_second, share_done))

    def residual(g, acc, ag):
        r = rows_of(g)
        nr, ni = total_of(g)
        re = R[0, r, :] - (0.5 * X0[0, r, :] + nr)
        im = R[1, r, :] - (0.5 * X0[1, r, :] + ni)
        R[0, r, :] = re
        R[1, r, :] = im
        put_low(re, im, g, xe1, ag)
        return acc + fold(re * re + im * im)

    acc = lax.fori_loop(0, 4, lambda g, a: residual(g, a, ag1), zero8)
    plan = gather(1, ag1)
    for s in plan[0]:
        s()
    rr = lax.fori_loop(4, NB, lambda g, a: residual(g, a, None), acc)
    halo_start(1, xe1)
    y_first, y_up, y_down, y_done = far_steps(1, xe1, far_r)
    y_first()
    rr = line(rr)

    apply(1, xe1, ag1, plan, (lambda: None, y_up, y_down, y_done))

    def image(g, acc):
        r = rows_of(g)
        nr, ni = total_of(g)
        vr, vi = R[0, r, :], R[1, r, :]
        wr, wi = 0.5 * vr + nr, 0.5 * vi + ni
        W[0, r, :] = wr
        W[1, r, :] = wi
        return acc[0] + fold(vr * wr + vi * wi), acc[1] + fold(vr * wi - vi * wr)

    pr, pi = lax.fori_loop(0, NB, image, (zero8, zero8))
    rr, pr, pi = clu_sum(0, [rr, line(pr), line(pi)])
    beta2 = rr + EPS
    h11r, h11i = pr / beta2, pi / beta2

    def ortho(g, acc, ag):
        r = rows_of(g)
        vr, vi = R[0, r, :], R[1, r, :]
        wr = W[0, r, :] - (h11r * vr - h11i * vi)
        wi = W[1, r, :] - (h11r * vi + h11i * vr)
        W[0, r, :] = wr
        W[1, r, :] = wi
        put_low(wr, wi, g, xe0, ag)
        return (acc[0] + fold(wr * wr + wi * wi), acc[1] + fold(vr * wr + vi * wi),
                acc[2] + fold(vr * wi - vi * wr))

    acc = lax.fori_loop(0, 4, lambda g, a: ortho(g, a, ag0), (zero8,) * 3)
    plan = gather(0, ag0)
    for s in plan[0]:
        s()
    ww, gr, gi = lax.fori_loop(4, NB, lambda g, a: ortho(g, a, None), acc)
    halo_start(0, xe0)
    y_first, y_up, y_down, y_done = far_steps(2, xe0, far_w)
    y_first()

    apply(0, xe0, ag0, plan, (lambda: None, y_up, y_down, y_done))

    def heights(g, acc):
        r = rows_of(g)
        nr, ni = total_of(g)
        vr, vi, wr, wi = R[0, r, :], R[1, r, :], W[0, r, :], W[1, r, :]
        ur, ui = 0.5 * wr + nr, 0.5 * wi + ni
        new = (vr * ur + vi * ui, vr * ui - vi * ur, wr * ur + wi * ui, wr * ui - wi * ur, ur * ur + ui * ui)
        return tuple(a + fold(n) for a, n in zip(acc, new))

    sums = lax.fori_loop(0, NB, heights, (zero8,) * 5)
    ww, gr, gi, ar, ai, br, bi, uu = clu_sum(1, [line(v) for v in (ww, gr, gi) + sums])

    beta = jnp.sqrt(beta2)
    inv_b = 1.0 / beta
    h21 = jnp.sqrt(ww / beta2 + EPS)
    scale2 = inv_b / h21
    n1, n2 = rr * (inv_b * inv_b), ww * (scale2 * scale2)
    cross = inv_b * scale2
    h12r, h12i, g12r, g12i = ar * cross, ai * cross, gr * cross, gi * cross
    sq2 = scale2 * scale2
    h22r, h22i, un = br * sq2, bi * sq2, uu * sq2
    m12, m22 = h12r * h12r + h12i * h12i, h22r * h22r + h22i * h22i
    mixr, mixi = h12r * h22r + h12i * h22i, h12r * h22i - h12i * h22r
    rest = un + m12 * (n1 - 2.0) + m22 * (n2 - 2.0) + 2.0 * (mixr * g12r - mixi * g12i)
    h32 = jnp.sqrt(jnp.maximum(rest, 0.0) + EPS)

    r_one = jnp.sqrt(h11r * h11r + h11i * h11i + h21 * h21)
    q_real, q_imag, q_low = h11r / r_one, h11i / r_one, h21 / r_one
    mix_real = q_real * h12r + q_imag * h12i + q_low * h22r
    mix_imag = q_real * h12i - q_imag * h12r + q_low * h22i
    top_real = h12r - (mix_real * q_real - mix_imag * q_imag)
    top_imag = h12i - (mix_real * q_imag + mix_imag * q_real)
    mid_real, mid_imag = h22r - mix_real * q_low, h22i - mix_imag * q_low
    r_two_sq = top_real**2 + top_imag**2 + mid_real**2 + mid_imag**2 + h32 * h32
    y2r, y2i = beta * top_real / r_two_sq, -beta * top_imag / r_two_sq
    y1r = (beta * q_real - (mix_real * y2r - mix_imag * y2i)) / r_one
    y1i = (-beta * q_imag - (mix_real * y2i + mix_imag * y2r)) / r_one
    a1r, a1i, a2r, a2i = y1r * inv_b, y1i * inv_b, y2r * scale2, y2i * scale2

    ones = jnp.ones((1, BLK), F32)
    blank = jnp.zeros((1, BLK), F32)
    gbuf[yy] = jnp.concatenate([a1r, a1i, a2r, a2i, own_pr * ones, own_pi * ones, blank, blank], axis=0)
    for d in (1, 2, 3):
        copy(gbuf.at[yy], gbuf.at[yy], g_send.at[0], g_recv.at[0], ydev(d)).start()

    def solve(g, carry):
        r = rows_of(g)
        vr, vi, wr, wi = R[0, r, :], R[1, r, :], W[0, r, :], W[1, r, :]
        X0[0, r, :] = X0[0, r, :] + (a1r * vr - a1i * vi) + (a2r * wr - a2i * wi)
        X0[1, r, :] = X0[1, r, :] + (a1r * vi + a1i * vr) + (a2r * wi + a2i * wr)
        return carry

    lax.fori_loop(0, NB, solve, 0)
    out_scat = pltpu.make_async_copy(X0, scat_hbm, out_sem.at[0])
    out_scat.start()
    three = gbuf.at[pl.ds(0, 3)]
    copy(three, three, g_send.at[0], g_recv.at[0], ydev(1)).wait()

    own_cr, own_ci = coef(yy, yy, own_pr, own_pi)
    factors = []
    for d in (-1, 1, 2):
        f = add4(yy, d)
        b = gbuf[f]
        cr, ci = coef(yy, f, b[4:5, :], b[5:6, :])
        for k in (0, 2):
            er, ei = b[k:k + 1, :], b[k + 1:k + 2, :]
            factors.append((cr * er + ci * ei, ci * er - cr * ei))

    def trace(g, carry):
        r = rows_of(g)
        t = full_in[0, r, :] + full_in[1, r, :] + (own_cr * X0[0, r, :] + own_ci * X0[1, r, :])
        for i in range(3):
            for k, store in enumerate((far_r, far_w)):
                v = store[i, g].astype(F32)
                fr, fi = factors[2 * i + k]
                t = t + (fr * v[:, :BLK] + fi * v[:, BLK:])
        part2[r, :] = t
        return carry

    lax.fori_loop(0, NB, trace, 0)
    out_trace = pltpu.make_async_copy(part2, trace_hbm, out_sem.at[1])
    out_trace.start()
    out_scat.wait()
    out_trace.wait()


def local(incident, initial, near_blocks, near_pattern, crack_blocks, crack_cluster, crack_source, crack_target, pulse):
    vmem, dma = pltpu.VMEM, pltpu.SemaphoreType.DMA
    hbm, smem = pl.BlockSpec(memory_space=pl.ANY), pl.BlockSpec(memory_space=pltpu.SMEM)
    vec = (2, PANELS, BLK)
    scratch = [
        vmem((NB * NEAR, 2 * BLK, BLK), BF16),
        vmem((EDGES, 2 * BLK, BLK), BF16),
        vmem(vec, F32), vmem(vec, F32), vmem(vec, F32), vmem(vec, F32),
        vmem((EDGES + 1, BLK, 2 * BLK), F32),
        vmem((3 * NB, BLK, 2 * BLK), BF16), vmem((3 * NB, BLK, 2 * BLK), BF16),
        vmem((32 * SET, HALF, 2 * BLK), BF16), vmem((32 * SET, HALF, 2 * BLK), BF16),
        vmem((PANELS, BLK), F32), vmem((PANELS, BLK), F32), vmem((PANELS, BLK), F32),
        vmem((2, PANELS // 2, BLK), F32), vmem((2, PANELS, BLK), F32),
        vmem((3, NB, BLK, 2 * BLK), BF16), vmem((3, NB, BLK, 2 * BLK), BF16),
        vmem((2, 8, 8, BLK), F32), vmem((2, 4, 8, BLK), F32), vmem((4, 8, BLK), F32),
        dma((4,)), dma((2,)), dma((2, 44)), dma((2,)), dma((2,)), dma((2, 2)), dma((2,)),
        dma((3, 4)), dma((4,)), dma((2,)), dma((2,)), dma((2,)), dma((2,)), dma((1,)), dma((1,)),
    ]
    place = jnp.arange(EDGES + NB, dtype=I32)
    target = jnp.where(place < EDGES, jnp.pad(crack_target, (0, NB)), place - EDGES)
    each = jnp.arange(EDGES, dtype=I32)
    found = (crack_target[None, :] == target[:, None]) & (each[None, :] < place[:, None])
    links = jnp.max(jnp.where(found, each[None, :], -1), axis=1)
    links = jnp.where(links < 0, EDGES, links)
    scattered, trace = pl.pallas_call(
        kernel,
        out_shape=(jax.ShapeDtypeStruct(vec, F32), jax.ShapeDtypeStruct((PANELS, BLK), F32)),
        in_specs=[smem] * 5 + [hbm] * 4,
        out_specs=(hbm, hbm),
        scratch_shapes=scratch,
        compiler_params=pltpu.CompilerParams(
            collective_id=0, has_side_effects=True, vmem_limit_bytes=66_000_000),
        name="gmres",
    )(
        near_pattern, crack_cluster, crack_source, links, pulse,
        incident.reshape(vec), initial.reshape(vec),
        near_blocks.reshape(NB * NEAR, 2 * BLK, BLK), crack_blocks.reshape(EDGES, 2 * BLK, BLK),
    )
    return scattered[None], trace[None]


def solution(mesh):
    in_specs = (
        P("frq", None, "clu", None),
        P("frq", None, "clu", None),
        P("clu", None, "frq", None, None, None),
        P("clu", None),
        P("clu", "frq", None, None, None),
        P("clu", None),
        P("clu"),
        P("clu"),
        P("frq", None),
    )
    out_specs = (P("frq", None, "clu", None), P("frq", "clu", None))
    return jax.shard_map(local, mesh=mesh, in_specs=in_specs, out_specs=out_specs, check_vma=False)
```

time: 831 us -> 221 us (0.27)
  blocking collectives: 320 us -> 0 us
  waiting for transfers between devices: 225 us -> 0 us
  Pallas kernels: 0 us -> 211 us
  local copies, waits for them, and re-layouts: 92.1 us -> 6.8 us
  other arithmetic: 86.8 us -> 1.89 us
  matrix products: 56.2 us -> 0 us
  starting transfers between devices: 31.4 us -> 0 us
  between operations: 14.9 us -> 0.65 us
    psum x5 -> x0, blocking collectives: 320 us -> none  [the longest x2 128 us: project(): summed = lax.psum(tuple(terms), 'clu')]
    pallas_call x0 -> x1, Pallas kernels: none -> 211 us  [local(): pl.pallas_call(kernel, out_shape=(jax.ShapeDtypeStruct(vec, F32), jax.Sha...]
    ppermute x6 -> x0, waiting for transfers between devices: 176 us -> none  [the longest x3 169 us: with_halo(): lax.ppermute(lax.slice_in_dim(block, block.shape[dim] - width, None, axis...]
    dot_general x12 -> x0, matrix products: 56.2 us -> none  [the longest x3 30.1 us: apply(): jnp.einsum('bsfcpq,fdbsqk->fcdbpk', near_blocks, columns, preferred_eleme...]
    gather x9 -> x0, local copies, waits for them, and re-layouts: 47.4 us -> none  [the longest x3 25.4 us: apply(): jnp.take(extended, near_flat, axis=2)]
    reduce_scatter x1 -> x0, waiting for transfers between devices: 43.3 us -> none  [local(): lax.psum_scatter(term + jnp.einsum('tf,fpk->tpk', coef_imag, scattered[:,...]
    select_n x8 -> x2, other arithmetic: 36 us -> 1.14 us  [the longest x1 0.66 us: local(): jnp.where(place < EDGES, jnp.pad(crack_target, (0, NB)), place - EDGES)]
    all_to_all x4 -> x0, starting transfers between devices: 26.2 us -> none  [the longest x3 16.8 us: fetch(): lax.all_to_all(picked, 'clu', split_axis=2, concat_axis=2, tiled=True)]
  transfers between devices with their start and end apart: 11 -> 0, of which waited for: 8 -> 0; matrix products, arithmetic and copies ran while one was open for 11% -> 0% of each run, Pallas kernels for 0% -> 0%
where the time goes in v1:
time: 221 us
  Pallas kernels  211 us (95%)
  local copies, waits for them, and re-layouts  6.8 us (3%)
    pallas_call x1, Pallas kernels, local(): pl.pallas_call(kernel, out_shape=(jax.ShapeDtypeStruct(vec, F32), jax.Sha...  211 us
    unnamed x6, local copies, waits for them, and re-layouts  6.8 us

profile of v1, /device:TPU:1, one launch (start us, length us, event | category | flops | bytes accessed | tf_op | source)
XLA Modules:
  0.0 220.7 jit_solution(4998205511558988420)
XLA Ops:
  0.6 0.7 compare_select_fusion.1
  1.3 0.7 select_reduce_fusion
  2.0 0.5 compare_select_fusion.links
  2.5 1.4 copy.13.pat
  3.9 1.3 copy.14.ccl
  5.2 211.3 %gmres.1 = (f32[2,2048,128]{2,1,0:T(8,128)}, f32[2048,128]{1,0:T(8,128)}) custom-call(s32[16,8]{1,0:T(8,128)} %copy.13.pat, s32[32,1]{1,0:T(8,128)} %copy.14.ccl, s32[32]{0:T(128)} %csrc.1, s32[48]{0:T(128)} %compare_select_fusion.links, f32[1,2]{1,0:T(1,128)} %pulse.1, f32[2,2048,128]{2,1,0:T(8,128)} %bitcast.7, f32[2,2048,128]{2,1,0:T(8,128)} %bitcast.8, ...), custom_call_target="tpu_custom_call" | custom-call | tf_op jit(solution)/shard_map/gmres/pallas_call | solution.py:557
  216.5 0.0 copy-start
  216.6 3.1 %copy.17 = f32[1,2,2048,128]{3,2,1,0:T(8,128)} copy(f32[1,2,2048,128]{3,2,1,0:T(8,128)} %bitcast.10) | data formatting | bytes 4194304
  219.7 0.0 copy-done
  219.7 1.0 copy.18
Async XLA Ops:
  216.5 3.1 %copy-start = (f32[2048,128]{1,0:T(8,128)S(1)}, f32[2048,128]{1,0:T(8,128)}, u32[]{:S(2)}) copy-start(f32[2048,128]{1,0:T(8,128)} %get-tuple-element.5) | copy-start | bytes 3145732

commit v2 on v1

--- a/solution.py
+++ b/solution.py
@@ -18,7 +18,8 @@
 SET = 8
 PANELS = NB * BLK
 NX = NZ = NY = 4
-SPLIT = 6
+PIECES = 4
+SPLIT = 4
 
 
 def add4(a, d):
@@ -166,7 +167,8 @@
         early = [primary(1), primary(-1)]
         early += [second(0, 1), second(0, -1)]
         middle = [second(1, 1), second(1, -1), second(2, 1), second(2, -1), far(1), far(-1)]
-        late = [second_far(1, 1), second_far(2, -1), second_far(1, -1), second_far(2, 1)]
+        middle += [second_far(1, 1), second_far(2, -1)]
+        late = [second_far(1, -1), second_far(2, 1)]
         late += [final(k, s) for k in range(4) for s in (1, -1)]
         return first, early, middle, late
 
@@ -188,10 +190,12 @@
 
         return firsts, mixed, finish, drain
 
-    def halo_start(parity, xe):
-        own = xe.at[pl.ds(NB, NB)]
-        copy(own, xe.at[pl.ds(0, NB)], halo_send.at[parity], halo_recv.at[parity, 0], dev(right)).start()
-        copy(own, xe.at[pl.ds(2 * NB, NB)], halo_send.at[parity], halo_recv.at[parity, 1], dev(left)).start()
+    def halo_start(parity, xe, piece):
+        size = NB // PIECES
+        own = xe.at[pl.ds(NB + piece * size, size)]
+        for side, start, target in ((0, 0, right), (1, 2 * NB, left)):
+            there = xe.at[pl.ds(start + piece * size, size)]
+            copy(own, there, halo_send.at[parity], halo_recv.at[parity, side], dev(target)).start()
 
     def halo_wait(parity, xe):
         arrived(xe.at[pl.ds(0, NB)], halo_send.at[parity], halo_recv.at[parity, 0], dev(left))
@@ -214,7 +218,7 @@
                         s()
             acc = None
             for p in range(NEAR // 2):
-                xs = jnp.concatenate([xe[pat[g, 2 * p]], xe[pat[g, 2 * p + 1]]], axis=0)
+                xs = jnp.concatenate([xe[pat[2 * p, g]], xe[pat[2 * p + 1, g]]], axis=0)
                 ms = jnp.concatenate([A[g * NEAR + 2 * p], A[g * NEAR + 2 * p + 1]], axis=1)
                 d = jnp.dot(ms, xs, preferred_element_type=F32)
                 acc = d if acc is None else acc + d
@@ -227,7 +231,7 @@
 
     def crack_products(ag):
         def edge(e, carry):
-            q = ccl[e, 0] * 4 + csrc[e]
+            q = ccl[0, e] * 4 + csrc[e]
             xc = jnp.concatenate([ag[2 * q], ag[2 * q + 1]], axis=0)
             turned = jnp.concatenate([-xc[:, BLK:], xc[:, :BLK]], axis=1)
             xs = jnp.concatenate([xc, turned], axis=0)
@@ -255,18 +259,24 @@
         rowbuf[k, spot] = jnp.concatenate(lines + pad, axis=0)
         for i in range(1, 8):
             copy(rowbuf.at[k, spot], rowbuf.at[k, spot], row_send.at[k], row_recv.at[k], row_peer(i)).start()
-        seven = rowbuf.at[k, pl.ds(0, 7)]
-        copy(seven, seven, row_send.at[k], row_recv.at[k], row_peer(1)).wait()
-        s = rowbuf[k, 0]
-        for i in range(1, 8):
-            s = s + rowbuf[k, i]
-        colbuf[k, zz] = s
-        for d in (1, 2, 3):
-            copy(colbuf.at[k, zz], colbuf.at[k, zz], col_send.at[k], col_recv.at[k], dev(clu(0, d))).start()
-        three = colbuf.at[k, pl.ds(0, 3)]
-        copy(three, three, col_send.at[k], col_recv.at[k], dev(clu(0, 1))).wait()
-        s = (colbuf[k, 0] + colbuf[k, 1]) + (colbuf[k, 2] + colbuf[k, 3])
-        return [s[i:i + 1, :] for i in range(len(lines))]
+
+        def cols():
+            seven = rowbuf.at[k, pl.ds(0, 7)]
+            copy(seven, seven, row_send.at[k], row_recv.at[k], row_peer(1)).wait()
+            s = rowbuf[k, 0]
+            for i in range(1, 8):
+                s = s + rowbuf[k, i]
+            colbuf[k, zz] = s
+            for d in (1, 2, 3):
+                copy(colbuf.at[k, zz], colbuf.at[k, zz], col_send.at[k], col_recv.at[k], dev(clu(0, d))).start()
+
+        def end():
+            three = colbuf.at[k, pl.ds(0, 3)]
+            copy(three, three, col_send.at[k], col_recv.at[k], dev(clu(0, 1))).wait()
+            s = (colbuf[k, 0] + colbuf[k, 1]) + (colbuf[k, 2] + colbuf[k, 3])
+            return [s[i:i + 1, :] for i in range(len(lines))]
+
+        return cols, end
 
     def far_steps(k, xe, dest):
         own = xe.at[pl.ds(NB, NB)]
@@ -288,8 +298,6 @@
         def done():
             arrived(dest.at[2, pl.ds(0, NB // 2)], y_send.at[k], y_recv.at[k, 2], ydev(-1))
             arrived(dest.at[2, pl.ds(NB // 2, NB // 2)], y_send.at[k], y_recv.at[k, 3], ydev(1))
-            for i in (0, 1):
-                pass
             r = dest.at[pl.ds(0, 3)]
             copy(r, r, y_send.at[k], y_recv.at[k, 0], ydev(1)).wait_send()
 
@@ -343,17 +351,21 @@
         copy(part2, part2, y_send.at[0], y_recv.at[0, 0], ydev(1)).wait_send()
         copy(full_in, full_in, y_send.at[3], y_recv.at[0, 0], ydev(1)).wait_send()
 
-    def apply(parity, xe, ag, plan, y_steps):
+    def apply(parity, xe, ag, plan, between):
         firsts, mixed, finish, drain = plan
         early, middle, late = mixed
-        for s in early:
+        n = 0
+        for i, s in enumerate(early):
             s()
-        for s in y_steps[:1]:
-            s()
+            if i % 2 and n < PIECES - 1:
+                n += 1
+                halo_start(parity, xe, n)
         for s in middle:
             s()
         halo_wait(parity, xe)
-        near_products(xe, late + list(y_steps[1:]))
+        near_products(xe, late)
+        for s in between:
+            s()
         finish()
         crack_products(ag)
         drain()
@@ -377,7 +389,7 @@
     for s in plan[0]:
         s()
     lax.fori_loop(4, NB, low_rest, 0)
-    halo_start(0, xe0)
+    halo_start(0, xe0, 0)
     share_first()
 
     prod[EDGES] = jnp.zeros((BLK, 2 * BLK), F32)
@@ -385,7 +397,7 @@
     loads[2].wait()
     loads[3].wait()
 
-    apply(0, xe0, ag0, plan, (share_second, share_done))
+    apply(0, xe0, ag0, plan, (share_second,))
 
     def residual(g, acc, ag):
         r = rows_of(g)
@@ -402,59 +414,55 @@
     for s in plan[0]:
         s()
     rr = lax.fori_loop(4, NB, lambda g, a: residual(g, a, None), acc)
-    halo_start(1, xe1)
-    y_first, y_up, y_down, y_done = far_steps(1, xe1, far_r)
+    halo_start(1, xe1, 0)
+    y_first, y_up, y_down, r_done = far_steps(1, xe1, far_r)
     y_first()
     rr = line(rr)
 
-    apply(1, xe1, ag1, plan, (lambda: None, y_up, y_down, y_done))
-
-    def image(g, acc):
+    apply(1, xe1, ag1, plan, (y_up, y_down))
+
+    def image(g, acc, ag):
         r = rows_of(g)
         nr, ni = total_of(g)
         vr, vi = R[0, r, :], R[1, r, :]
         wr, wi = 0.5 * vr + nr, 0.5 * vi + ni
         W[0, r, :] = wr
         W[1, r, :] = wi
+        put_low(wr, wi, g, xe0, ag)
         return acc[0] + fold(vr * wr + vi * wi), acc[1] + fold(vr * wi - vi * wr)
 
-    pr, pi = lax.fori_loop(0, NB, image, (zero8, zero8))
-    rr, pr, pi = clu_sum(0, [rr, line(pr), line(pi)])
-    beta2 = rr + EPS
-    h11r, h11i = pr / beta2, pi / beta2
-
-    def ortho(g, acc, ag):
-        r = rows_of(g)
-        vr, vi = R[0, r, :], R[1, r, :]
-        wr = W[0, r, :] - (h11r * vr - h11i * vi)
-        wi = W[1, r, :] - (h11r * vi + h11i * vr)
-        W[0, r, :] = wr
-        W[1, r, :] = wi
-        put_low(wr, wi, g, xe0, ag)
-        return (acc[0] + fold(wr * wr + wi * wi), acc[1] + fold(vr * wr + vi * wi),
-                acc[2] + fold(vr * wi - vi * wr))
-
-    acc = lax.fori_loop(0, 4, lambda g, a: ortho(g, a, ag0), (zero8,) * 3)
+    acc = lax.fori_loop(0, 4, lambda g, a: image(g, a, ag0), (zero8,) * 2)
     plan = gather(0, ag0)
     for s in plan[0]:
         s()
-    ww, gr, gi = lax.fori_loop(4, NB, lambda g, a: ortho(g, a, None), acc)
-    halo_start(0, xe0)
-    y_first, y_up, y_down, y_done = far_steps(2, xe0, far_w)
+    pr, pi = lax.fori_loop(4, NB, lambda g, a: image(g, a, None), acc)
+    halo_start(0, xe0, 0)
+    sum_cols, sum_end = clu_sum(0, [rr, line(pr), line(pi)])
+    y_first, y_up, y_down, w_done = far_steps(2, xe0, far_w)
     y_first()
 
-    apply(0, xe0, ag0, plan, (lambda: None, y_up, y_down, y_done))
+    apply(0, xe0, ag0, plan, (y_up, y_down, sum_cols))
+    rr, pr, pi = sum_end()
+    beta2 = rr + EPS
+    h11r, h11i = pr / beta2, pi / beta2
 
     def heights(g, acc):
         r = rows_of(g)
         nr, ni = total_of(g)
         vr, vi, wr, wi = R[0, r, :], R[1, r, :], W[0, r, :], W[1, r, :]
-        ur, ui = 0.5 * wr + nr, 0.5 * wi + ni
-        new = (vr * ur + vi * ui, vr * ui - vi * ur, wr * ur + wi * ui, wr * ui - wi * ur, ur * ur + ui * ui)
+        ur = 0.5 * wr + nr - (h11r * wr - h11i * wi)
+        ui = 0.5 * wi + ni - (h11r * wi + h11i * wr)
+        wr, wi = wr - (h11r * vr - h11i * vi), wi - (h11r * vi + h11i * vr)
+        W[0, r, :] = wr
+        W[1, r, :] = wi
+        new = (wr * wr + wi * wi, vr * wr + vi * wi, vr * wi - vi * wr,
+               vr * ur + vi * ui, vr * ui - vi * ur, wr * ur + wi * ui, wr * ui - wi * ur, ur * ur + ui * ui)
         return tuple(a + fold(n) for a, n in zip(acc, new))
 
-    sums = lax.fori_loop(0, NB, heights, (zero8,) * 5)
-    ww, gr, gi, ar, ai, br, bi, uu = clu_sum(1, [line(v) for v in (ww, gr, gi) + sums])
+    sums = lax.fori_loop(0, NB, heights, (zero8,) * 8)
+    sum_cols, sum_end = clu_sum(1, [line(v) for v in sums])
+    sum_cols()
+    ww, gr, gi, ar, ai, br, bi, uu = sum_end()
 
     beta = jnp.sqrt(beta2)
     inv_b = 1.0 / beta
@@ -485,7 +493,8 @@
 
     ones = jnp.ones((1, BLK), F32)
     blank = jnp.zeros((1, BLK), F32)
-    gbuf[yy] = jnp.concatenate([a1r, a1i, a2r, a2i, own_pr * ones, own_pi * ones, blank, blank], axis=0)
+    b1r, b1i = a1r - (a2r * h11r - a2i * h11i), a1i - (a2r * h11i + a2i * h11r)
+    gbuf[yy] = jnp.concatenate([b1r, b1i, a2r, a2i, own_pr * ones, own_pi * ones, blank, blank], axis=0)
     for d in (1, 2, 3):
         copy(gbuf.at[yy], gbuf.at[yy], g_send.at[0], g_recv.at[0], ydev(d)).start()
 
@@ -499,6 +508,9 @@
     lax.fori_loop(0, NB, solve, 0)
     out_scat = pltpu.make_async_copy(X0, scat_hbm, out_sem.at[0])
     out_scat.start()
+    share_done()
+    r_done()
+    w_done()
     three = gbuf.at[pl.ds(0, 3)]
     copy(three, three, g_send.at[0], g_recv.at[0], ydev(1)).wait()
 
@@ -564,7 +576,7 @@
             collective_id=0, has_side_effects=True, vmem_limit_bytes=66_000_000),
         name="gmres",
     )(
-        near_pattern, crack_cluster, crack_source, links, pulse,
+        near_pattern.T, crack_cluster.T, crack_source, links, pulse,
         incident.reshape(vec), initial.reshape(vec),
         near_blocks.reshape(NB * NEAR, 2 * BLK, BLK), crack_blocks.reshape(EDGES, 2 * BLK, BLK),
     )

time: 221 us -> 172 us (0.78)
  Pallas kernels: 211 us -> 164 us
  local copies, waits for them, and re-layouts: 6.8 us -> 4.11 us
    pallas_call x1, Pallas kernels: 211 us -> 164 us  [local(): pl.pallas_call(kernel, out_shape=(jax.ShapeDtypeStruct(vec, F32), jax.Sha...]
    unnamed x6 -> x4, local copies, waits for them, and re-layouts: 6.8 us -> 4.11 us
where the time goes in v2:
time: 172 us; the launch traced here: 171 us
  Pallas kernels  164 us (95%)
  local copies, waits for them, and re-layouts  4.11 us (2%)
  other arithmetic  1.92 us (1%)
    pallas_call x1, Pallas kernels, local(): pl.pallas_call(kernel, out_shape=(jax.ShapeDtypeStruct(vec, F32), jax.Sha...  164 us
    unnamed x4, local copies, waits for them, and re-layouts  4.11 us

profile of v2, /device:TPU:1, one launch (start us, length us, event | category | flops | bytes accessed | tf_op | source)
XLA Modules:
  0.0 171.1 jit_solution(13149755272169361330)
XLA Ops:
  0.6 0.7 compare_select_fusion.1
  1.3 0.7 select_reduce_fusion
  2.0 0.5 compare_select_fusion.links
  2.5 164.5 %gmres.1 = (f32[2,2048,128]{2,1,0:T(8,128)}, f32[2048,128]{1,0:T(8,128)}) custom-call(s32[8,16]{1,0:T(8,128)} %bitcast.14, s32[1,32]{1,0:T(1,128)} %bitcast.15, s32[32]{0:T(128)} %csrc.1, s32[48]{0:T(128)} %compare_select_fusion.links, f32[1,2]{1,0:T(1,128)} %pulse.1, f32[2,2048,128]{2,1,0:T(8,128)} %bitcast.10, f32[2,2048,128]{2,1,0:T(8,128)} %bitcast.11, ...), custom_call_target="tpu_custom_call" | custom-call | tf_op jit(solution)/shard_map/gmres/pallas_call | solution.py:569
  167.0 0.0 copy-start
  167.0 3.1 %copy.13 = f32[1,2,2048,128]{3,2,1,0:T(8,128)} copy(f32[1,2,2048,128]{3,2,1,0:T(8,128)} %bitcast.9) | data formatting | bytes 4194304
  170.2 0.0 copy-done
  170.2 1.0 copy.14
Async XLA Ops:
  167.0 3.1 %copy-start = (f32[2048,128]{1,0:T(8,128)S(1)}, f32[2048,128]{1,0:T(8,128)}, u32[]{:S(2)}) copy-start(f32[2048,128]{1,0:T(8,128)} %get-tuple-element.5) | copy-start | bytes 3145732

commit v3 on v2

--- a/solution.py
+++ b/solution.py
@@ -16,9 +16,11 @@
 EDGES = 32
 HALF = BLK // 2
 SET = 8
+SPAN = 2 * NB
 PANELS = NB * BLK
 NX = NZ = NY = 4
-PIECES = 4
+PIECES = 3
+MIDWAY = 12
 SPLIT = 4
 
 
@@ -30,8 +32,8 @@
     pat, ccl, csrc, links, pulse, inc_hbm, ini_hbm, near_hbm, crack_hbm,
     scat_hbm, trace_hbm,
     A, C, R, X0, W, Y, prod, xe0, xe1, ag0, ag1,
-    part2, sendp, sendm, half_in, full_in, far_r, far_w,
-    rowbuf, colbuf, gbuf,
+    part2, sendp, sendm, half_in, full_in, far_r, far_w, fine, far_f,
+    rowbuf, colbuf, gbuf, allbuf,
     load_sem, out_sem, ag_recv, ag_send, pair_recv, halo_recv, halo_send,
     y_recv, y_send, row_recv, row_send, col_recv, col_send, g_recv, g_send,
 ):
@@ -44,6 +46,7 @@
         return (add4(zz, dz) * 4 + add4(xx, dx)) * 2 + core
 
     partner = me + 1 - 2 * core
+    beyond = lax.rem(me + jnp.where(core == 1, 30, 2), 32)
     right, left = lax.rem(me + 1, 32), lax.rem(me + 31, 32)
 
     def dev(c):
@@ -70,10 +73,8 @@
     for l in loads:
         l.start()
     barrier = pltpu.get_barrier_semaphore()
-    peers = [row_peer(i) for i in range(1, 8)]
-    peers += [dev(clu(0, d)) for d in (1, 2, 3)]
+    peers = [dev(lax.rem(me + i, 32)) for i in range(1, 32)]
     peers += [ydev(d) for d in (1, 2, 3)]
-    peers += [dev(right), dev(left)]
     for p in peers:
         pl.semaphore_signal(barrier, inc=1, device_id=p, device_id_type=MESH)
 
@@ -82,11 +83,12 @@
 
     def put_low(re, im, g, xe, ag):
         low = jnp.concatenate([re.astype(BF16), im.astype(BF16)], axis=1)
-        xe[NB + g] = low
+        low = low.reshape(2, HALF, 2 * BLK)
+        xe[pl.ds(2 * (NB + g), 2)] = low
         if ag is not None:
-            ag[pl.ds(me * SET + 2 * g, 2)] = low.reshape(2, HALF, 2 * BLK)
-
-    def gather_steps(parity, ag, group, off, n, x_first):
+            ag[pl.ds(me * SET + 2 * g, 2)] = low
+
+    def gather_steps(parity, ag, xe, group, off, n, x_first):
         hn = n // 2
         base = 22 * group
 
@@ -107,6 +109,12 @@
         def share(c, part):
             r = region(c, part)
             copy(r, r, ag_send.at[parity], pair_recv.at[parity], dev(partner)).start()
+
+        def to_halo(c):
+            @pl.when(c == beyond)
+            def _():
+                there = xe.at[pl.ds(2 * SPAN * (1 - core) + off, n)]
+                copy(region(c, 0), there, halo_send.at[parity], halo_recv.at[parity, 1 - core], dev(partner)).start()
 
         cols = [0, -1, 1]
 
@@ -126,6 +134,8 @@
                 send(c, 0, at(0, 1), 4 + 4 * k)
                 send(c, 0, at(0, -1), 5 + 4 * k)
                 share(c, 0)
+                if x_first:
+                    to_halo(c)
             return step
 
         def far(sign):
@@ -144,6 +154,8 @@
                 wait(c, 0, at(0, -sign), 4 + 4 * k + (0 if sign > 0 else 1))
                 send(c, 1 if sign > 0 else 2, at(0, sign), 6 + 4 * k + (0 if sign > 0 else 1))
                 share(c, 0)
+                if (k == 0 and not x_first) or (k, sign) in ((1, 1), (2, -1)):
+                    to_halo(c)
             return step
 
         def second_far(part, sign):
@@ -172,9 +184,9 @@
         late += [final(k, s) for k in range(4) for s in (1, -1)]
         return first, early, middle, late
 
-    def gather(parity, ag):
+    def gather(parity, ag, xe):
         groups = [(0, SPLIT, True), (SPLIT, SET - SPLIT, False)]
-        made = [gather_steps(parity, ag, i, *g) for i, g in enumerate(groups) if g[1]]
+        made = [gather_steps(parity, ag, xe, i, *g) for i, g in enumerate(groups) if g[1]]
         firsts = [m[0] for m in made]
         mixed = [[s for steps in zip(*[m[k] for m in made]) for s in steps] for k in (1, 2, 3)]
         total = 0
@@ -191,18 +203,23 @@
         return firsts, mixed, finish, drain
 
     def halo_start(parity, xe, piece):
-        size = NB // PIECES
-        own = xe.at[pl.ds(NB + piece * size, size)]
-        for side, start, target in ((0, 0, right), (1, 2 * NB, left)):
-            there = xe.at[pl.ds(start + piece * size, size)]
-            copy(own, there, halo_send.at[parity], halo_recv.at[parity, side], dev(target)).start()
+        size = (SPAN - SET) // PIECES
+        first = SET + piece * size
+        own = xe.at[pl.ds(SPAN + first, size)]
+        for k, target in ((0, right), (1, left)):
+            there = xe.at[pl.ds(2 * SPAN * k + first, size)]
+            copy(own, there, halo_send.at[parity], halo_recv.at[parity, k], dev(target)).start()
+
+    def halo_fronts(parity, xe):
+        there = xe.at[pl.ds(2 * SPAN * core, SET)]
+        copy(xe.at[pl.ds(SPAN, SET)], there, halo_send.at[parity], halo_recv.at[parity, core], dev(partner)).start()
 
     def halo_wait(parity, xe):
-        arrived(xe.at[pl.ds(0, NB)], halo_send.at[parity], halo_recv.at[parity, 0], dev(left))
-        arrived(xe.at[pl.ds(2 * NB, NB)], halo_send.at[parity], halo_recv.at[parity, 1], dev(right))
+        for k, source in ((0, left), (1, right)):
+            arrived(xe.at[pl.ds(2 * SPAN * k, SPAN)], halo_send.at[parity], halo_recv.at[parity, k], dev(source))
 
     def halo_drain(parity, xe):
-        r = xe.at[pl.ds(0, 2 * NB)]
+        r = xe.at[pl.ds(0, 2 * SPAN)]
         copy(r, r, halo_send.at[parity], halo_recv.at[parity, 0], dev(right)).wait_send()
 
     def near_products(xe, steps):
@@ -218,7 +235,8 @@
                         s()
             acc = None
             for p in range(NEAR // 2):
-                xs = jnp.concatenate([xe[pat[2 * p, g]], xe[pat[2 * p + 1, g]]], axis=0)
+                a, b = 2 * pat[2 * p, g], 2 * pat[2 * p + 1, g]
+                xs = jnp.concatenate([xe[a], xe[a + 1], xe[b], xe[b + 1]], axis=0)
                 ms = jnp.concatenate([A[g * NEAR + 2 * p], A[g * NEAR + 2 * p + 1]], axis=1)
                 d = jnp.dot(ms, xs, preferred_element_type=F32)
                 acc = d if acc is None else acc + d
@@ -239,7 +257,7 @@
             prod[e] = jnp.dot(ms, xs, preferred_element_type=F32) + prod[links[e]]
             return carry
 
-        lax.fori_loop(0, EDGES, edge, 0)
+        lax.fori_loop(0, EDGES, edge, 0, unroll=8)
 
     def total_of(g):
         r = rows_of(g)
@@ -279,7 +297,7 @@
         return cols, end
 
     def far_steps(k, xe, dest):
-        own = xe.at[pl.ds(NB, NB)]
+        own = xe.at[pl.ds(SPAN, SPAN)]
 
         def first():
             copy(own, dest.at[0], y_send.at[k], y_recv.at[k, 0], ydev(1)).start()
@@ -287,17 +305,17 @@
 
         def up():
             arrived(dest.at[0], y_send.at[k], y_recv.at[k, 0], ydev(-1))
-            copy(dest.at[0, pl.ds(0, NB // 2)], dest.at[2, pl.ds(0, NB // 2)],
+            copy(dest.at[0, pl.ds(0, NB)], dest.at[2, pl.ds(0, NB)],
                  y_send.at[k], y_recv.at[k, 2], ydev(1)).start()
 
         def down():
             arrived(dest.at[1], y_send.at[k], y_recv.at[k, 1], ydev(1))
-            copy(dest.at[1, pl.ds(NB // 2, NB // 2)], dest.at[2, pl.ds(NB // 2, NB // 2)],
+            copy(dest.at[1, pl.ds(NB, NB)], dest.at[2, pl.ds(NB, NB)],
                  y_send.at[k], y_recv.at[k, 3], ydev(-1)).start()
 
         def done():
-            arrived(dest.at[2, pl.ds(0, NB // 2)], y_send.at[k], y_recv.at[k, 2], ydev(-1))
-            arrived(dest.at[2, pl.ds(NB // 2, NB // 2)], y_send.at[k], y_recv.at[k, 3], ydev(1))
+            arrived(dest.at[2, pl.ds(0, NB)], y_send.at[k], y_recv.at[k, 2], ydev(-1))
+            arrived(dest.at[2, pl.ds(NB, NB)], y_send.at[k], y_recv.at[k, 3], ydev(1))
             r = dest.at[pl.ds(0, 3)]
             copy(r, r, y_send.at[k], y_recv.at[k, 0], ydev(1)).wait_send()
 
@@ -342,16 +360,16 @@
             return carry
 
         lax.fori_loop(0, NB // 2, body, 0)
-        copy(sendp, full_in.at[0], y_send.at[3], y_recv.at[0, 2], ydev(1)).start()
-        copy(sendm, full_in.at[1], y_send.at[3], y_recv.at[0, 3], ydev(-1)).start()
+        copy(sendp, full_in.at[0], y_send.at[4], y_recv.at[0, 2], ydev(1)).start()
+        copy(sendm, full_in.at[1], y_send.at[4], y_recv.at[0, 3], ydev(-1)).start()
 
     def share_done():
-        arrived(full_in.at[0], y_send.at[3], y_recv.at[0, 2], ydev(-1))
-        arrived(full_in.at[1], y_send.at[3], y_recv.at[0, 3], ydev(1))
+        arrived(full_in.at[0], y_send.at[4], y_recv.at[0, 2], ydev(-1))
+        arrived(full_in.at[1], y_send.at[4], y_recv.at[0, 3], ydev(1))
         copy(part2, part2, y_send.at[0], y_recv.at[0, 0], ydev(1)).wait_send()
-        copy(full_in, full_in, y_send.at[3], y_recv.at[0, 0], ydev(1)).wait_send()
-
-    def apply(parity, xe, ag, plan, between):
+        copy(full_in, full_in, y_send.at[4], y_recv.at[0, 0], ydev(1)).wait_send()
+
+    def apply(parity, xe, ag, plan, mid, between):
         firsts, mixed, finish, drain = plan
         early, middle, late = mixed
         n = 0
@@ -360,7 +378,7 @@
             if i % 2 and n < PIECES - 1:
                 n += 1
                 halo_start(parity, xe, n)
-        for s in middle:
+        for s in middle[:MIDWAY] + list(mid) + middle[MIDWAY:]:
             s()
         halo_wait(parity, xe)
         near_products(xe, late)
@@ -385,10 +403,11 @@
 
     lax.fori_loop(0, 4, low_front, 0)
     pl.semaphore_wait(barrier, len(peers))
-    plan = gather(0, ag0)
+    plan = gather(0, ag0, xe0)
     for s in plan[0]:
         s()
     lax.fori_loop(4, NB, low_rest, 0)
+    halo_fronts(0, xe0)
     halo_start(0, xe0, 0)
     share_first()
 
@@ -397,7 +416,7 @@
     loads[2].wait()
     loads[3].wait()
 
-    apply(0, xe0, ag0, plan, (share_second,))
+    apply(0, xe0, ag0, plan, (share_second,), ())
 
     def residual(g, acc, ag):
         r = rows_of(g)
@@ -407,19 +426,30 @@
         R[0, r, :] = re
         R[1, r, :] = im
         put_low(re, im, g, xe1, ag)
+        less = [(v - v.astype(BF16).astype(F32)).astype(BF16) for v in (re, im)]
+        fine[pl.ds(2 * g, 2)] = jnp.concatenate(less, axis=1).reshape(2, HALF, 2 * BLK)
         return acc + fold(re * re + im * im)
 
     acc = lax.fori_loop(0, 4, lambda g, a: residual(g, a, ag1), zero8)
-    plan = gather(1, ag1)
+    plan = gather(1, ag1, xe1)
     for s in plan[0]:
         s()
     rr = lax.fori_loop(4, NB, lambda g, a: residual(g, a, None), acc)
+    halo_fronts(1, xe1)
     halo_start(1, xe1, 0)
     y_first, y_up, y_down, r_done = far_steps(1, xe1, far_r)
     y_first()
+    lo, hi = pl.ds(0, NB), pl.ds(NB, NB)
+    copy(fine.at[lo], far_f.at[lo], y_send.at[3], y_recv.at[3, 0], ydev(1)).start()
+    copy(fine.at[hi], far_f.at[hi], y_send.at[3], y_recv.at[3, 1], ydev(-1)).start()
+
+    def fine_done():
+        arrived(far_f.at[lo], y_send.at[3], y_recv.at[3, 0], ydev(-1))
+        arrived(far_f.at[hi], y_send.at[3], y_recv.at[3, 1], ydev(1))
+        copy(far_f, far_f, y_send.at[3], y_recv.at[3, 0], ydev(1)).wait_send()
+
     rr = line(rr)
-
-    apply(1, xe1, ag1, plan, (y_up, y_down))
+    apply(1, xe1, ag1, plan, (), (y_up, y_down))
 
     def image(g, acc, ag):
         r = rows_of(g)
@@ -432,16 +462,17 @@
         return acc[0] + fold(vr * wr + vi * wi), acc[1] + fold(vr * wi - vi * wr)
 
     acc = lax.fori_loop(0, 4, lambda g, a: image(g, a, ag0), (zero8,) * 2)
-    plan = gather(0, ag0)
+    plan = gather(0, ag0, xe0)
     for s in plan[0]:
         s()
     pr, pi = lax.fori_loop(4, NB, lambda g, a: image(g, a, None), acc)
+    halo_fronts(0, xe0)
     halo_start(0, xe0, 0)
     sum_cols, sum_end = clu_sum(0, [rr, line(pr), line(pi)])
     y_first, y_up, y_down, w_done = far_steps(2, xe0, far_w)
     y_first()
 
-    apply(0, xe0, ag0, plan, (y_up, y_down, sum_cols))
+    apply(0, xe0, ag0, plan, (), (sum_cols, y_up, y_down))
     rr, pr, pi = sum_end()
     beta2 = rr + EPS
     h11r, h11i = pr / beta2, pi / beta2
@@ -460,9 +491,16 @@
         return tuple(a + fold(n) for a, n in zip(acc, new))
 
     sums = lax.fori_loop(0, NB, heights, (zero8,) * 8)
-    sum_cols, sum_end = clu_sum(1, [line(v) for v in sums])
-    sum_cols()
-    ww, gr, gi, ar, ai, br, bi, uu = sum_end()
+    allbuf[me] = jnp.concatenate([line(v) for v in sums], axis=0)
+    for i in range(1, 32):
+        peer = dev(lax.rem(me + i, 32))
+        copy(allbuf.at[me], allbuf.at[me], col_send.at[1], col_recv.at[1], peer).start()
+    rest31 = allbuf.at[pl.ds(0, 31)]
+    copy(rest31, rest31, col_send.at[1], col_recv.at[1], dev(right)).wait()
+    terms = [allbuf[i] for i in range(32)]
+    while len(terms) > 1:
+        terms = [a + b for a, b in zip(terms[::2], terms[1::2])]
+    ww, gr, gi, ar, ai, br, bi, uu = [terms[0][i:i + 1, :] for i in range(8)]
 
     beta = jnp.sqrt(beta2)
     inv_b = 1.0 / beta
@@ -510,6 +548,7 @@
     out_scat.start()
     share_done()
     r_done()
+    fine_done()
     w_done()
     three = gbuf.at[pl.ds(0, 3)]
     copy(three, three, g_send.at[0], g_recv.at[0], ydev(1)).wait()
@@ -524,18 +563,24 @@
             er, ei = b[k:k + 1, :], b[k + 1:k + 2, :]
             factors.append((cr * er + ci * ei, ci * er - cr * ei))
 
-    def trace(g, carry):
+    def load_block(store, g):
+        return store[pl.ds(2 * g, 2)].reshape(BLK, 2 * BLK).astype(F32)
+
+    def trace(g, nearest):
         r = rows_of(g)
         t = full_in[0, r, :] + full_in[1, r, :] + (own_cr * X0[0, r, :] + own_ci * X0[1, r, :])
         for i in range(3):
             for k, store in enumerate((far_r, far_w)):
-                v = store[i, g].astype(F32)
+                v = load_block(store.at[i], g)
+                if k == 0 and i == nearest:
+                    v = v + load_block(far_f, g)
                 fr, fi = factors[2 * i + k]
                 t = t + (fr * v[:, :BLK] + fi * v[:, BLK:])
         part2[r, :] = t
-        return carry
-
-    lax.fori_loop(0, NB, trace, 0)
+        return 0
+
+    lax.fori_loop(0, NB // 2, lambda g, _: trace(g, 0), 0)
+    lax.fori_loop(NB // 2, NB, lambda g, _: trace(g, 1), 0)
     out_trace = pltpu.make_async_copy(part2, trace_hbm, out_sem.at[1])
     out_trace.start()
     out_scat.wait()
@@ -551,14 +596,15 @@
         vmem((EDGES, 2 * BLK, BLK), BF16),
         vmem(vec, F32), vmem(vec, F32), vmem(vec, F32), vmem(vec, F32),
         vmem((EDGES + 1, BLK, 2 * BLK), F32),
-        vmem((3 * NB, BLK, 2 * BLK), BF16), vmem((3 * NB, BLK, 2 * BLK), BF16),
+        vmem((3 * SPAN, HALF, 2 * BLK), BF16), vmem((3 * SPAN, HALF, 2 * BLK), BF16),
         vmem((32 * SET, HALF, 2 * BLK), BF16), vmem((32 * SET, HALF, 2 * BLK), BF16),
         vmem((PANELS, BLK), F32), vmem((PANELS, BLK), F32), vmem((PANELS, BLK), F32),
         vmem((2, PANELS // 2, BLK), F32), vmem((2, PANELS, BLK), F32),
-        vmem((3, NB, BLK, 2 * BLK), BF16), vmem((3, NB, BLK, 2 * BLK), BF16),
-        vmem((2, 8, 8, BLK), F32), vmem((2, 4, 8, BLK), F32), vmem((4, 8, BLK), F32),
+        vmem((3, SPAN, HALF, 2 * BLK), BF16), vmem((3, SPAN, HALF, 2 * BLK), BF16),
+        vmem((SPAN, HALF, 2 * BLK), BF16), vmem((SPAN, HALF, 2 * BLK), BF16),
+        vmem((1, 8, 8, BLK), F32), vmem((1, 4, 8, BLK), F32), vmem((4, 8, BLK), F32), vmem((32, 8, BLK), F32),
         dma((4,)), dma((2,)), dma((2, 44)), dma((2,)), dma((2,)), dma((2, 2)), dma((2,)),
-        dma((3, 4)), dma((4,)), dma((2,)), dma((2,)), dma((2,)), dma((2,)), dma((1,)), dma((1,)),
+        dma((4, 4)), dma((5,)), dma((2,)), dma((2,)), dma((2,)), dma((2,)), dma((1,)), dma((1,)),
     ]
     place = jnp.arange(EDGES + NB, dtype=I32)
     target = jnp.where(place < EDGES, jnp.pad(crack_target, (0, NB)), place - EDGES)

time: 172 us -> 153 us (0.89)
  Pallas kernels: 164 us -> 146 us
    pallas_call x1, Pallas kernels: 164 us -> 146 us  [local(): pl.pallas_call(kernel, out_shape=(jax.ShapeDtypeStruct(vec, F32), jax.Sha...]
where the time goes in v3:
time: 153 us
  Pallas kernels  146 us (95%)
  local copies, waits for them, and re-layouts  4.11 us (3%)
  other arithmetic  1.92 us (1%)
    pallas_call x1, Pallas kernels, local(): pl.pallas_call(kernel, out_shape=(jax.ShapeDtypeStruct(vec, F32), jax.Sha...  146 us
    unnamed x4, local copies, waits for them, and re-layouts  4.11 us

profile of v3, /device:TPU:1, one launch (start us, length us, event | category | flops | bytes accessed | tf_op | source)
XLA Modules:
  0.0 152.8 jit_solution(7117001949618502489)
XLA Ops:
  0.6 0.7 compare_select_fusion.1
  1.3 0.7 select_reduce_fusion
  2.0 0.5 compare_select_fusion.links
  2.5 146.1 %gmres.1 = (f32[2,2048,128]{2,1,0:T(8,128)}, f32[2048,128]{1,0:T(8,128)}) custom-call(s32[8,16]{1,0:T(8,128)} %bitcast.14, s32[1,32]{1,0:T(1,128)} %bitcast.15, s32[32]{0:T(128)} %csrc.1, s32[48]{0:T(128)} %compare_select_fusion.links, f32[1,2]{1,0:T(1,128)} %pulse.1, f32[2,2048,128]{2,1,0:T(8,128)} %bitcast.10, f32[2,2048,128]{2,1,0:T(8,128)} %bitcast.11, ...), custom_call_target="tpu_custom_call" | custom-call | tf_op jit(solution)/shard_map/gmres/pallas_call | solution.py:615
  148.7 0.0 copy-start
  148.7 3.1 %copy.13 = f32[1,2,2048,128]{3,2,1,0:T(8,128)} copy(f32[1,2,2048,128]{3,2,1,0:T(8,128)} %bitcast.9) | data formatting | bytes 4194304
  151.8 0.0 copy-done
  151.8 1.0 copy.14
Async XLA Ops:
  148.7 3.1 %copy-start = (f32[2048,128]{1,0:T(8,128)S(1)}, f32[2048,128]{1,0:T(8,128)}, u32[]{:S(2)}) copy-start(f32[2048,128]{1,0:T(8,128)} %get-tuple-element.5) | copy-start | bytes 3145732

commit v4 on v3

--- a/solution.py
+++ b/solution.py
@@ -177,9 +177,7 @@
             return step
 
         early = [primary(1), primary(-1)]
-        early += [second(0, 1), second(0, -1)]
-        middle = [second(1, 1), second(1, -1), second(2, 1), second(2, -1), far(1), far(-1)]
-        middle += [second_far(1, 1), second_far(2, -1)]
+        middle = [far(1), far(-1), second(0, 1), second(0, -1), second(1, 1), second(1, -1), second(2, 1), second(2, -1), second_far(1, 1), second_far(2, -1), ]
         late = [second_far(1, -1), second_far(2, 1)]
         late += [final(k, s) for k in range(4) for s in (1, -1)]
         return first, early, middle, late
@@ -386,8 +384,12 @@
             s()
         finish()
         crack_products(ag)
-        drain()
-        halo_drain(parity, xe)
+
+        def drained():
+            drain()
+            halo_drain(parity, xe)
+
+        return drained
 
     loads[0].wait()
 
@@ -416,7 +418,7 @@
     loads[2].wait()
     loads[3].wait()
 
-    apply(0, xe0, ag0, plan, (share_second,), ())
+    sent = apply(0, xe0, ag0, plan, (share_second,), ())
 
     def residual(g, acc, ag):
         r = rows_of(g)
@@ -431,6 +433,7 @@
         return acc + fold(re * re + im * im)
 
     acc = lax.fori_loop(0, 4, lambda g, a: residual(g, a, ag1), zero8)
+    sent()
     plan = gather(1, ag1, xe1)
     for s in plan[0]:
         s()
@@ -449,7 +452,7 @@
         copy(far_f, far_f, y_send.at[3], y_recv.at[3, 0], ydev(1)).wait_send()
 
     rr = line(rr)
-    apply(1, xe1, ag1, plan, (), (y_up, y_down))
+    sent_r = apply(1, xe1, ag1, plan, (), (y_up, y_down))
 
     def image(g, acc, ag):
         r = rows_of(g)
@@ -472,7 +475,7 @@
     y_first, y_up, y_down, w_done = far_steps(2, xe0, far_w)
     y_first()
 
-    apply(0, xe0, ag0, plan, (), (sum_cols, y_up, y_down))
+    sent_w = apply(0, xe0, ag0, plan, (), (sum_cols, y_up, y_down))
     rr, pr, pi = sum_end()
     beta2 = rr + EPS
     h11r, h11i = pr / beta2, pi / beta2
@@ -550,6 +553,8 @@
     r_done()
     fine_done()
     w_done()
+    sent_r()
+    sent_w()
     three = gbuf.at[pl.ds(0, 3)]
     copy(three, three, g_send.at[0], g_recv.at[0], ydev(1)).wait()
 

time: 153 us -> 146 us (0.954)
  Pallas kernels: 146 us -> 139 us
    pallas_call x1, Pallas kernels: 146 us -> 139 us  [local(): pl.pallas_call(kernel, out_shape=(jax.ShapeDtypeStruct(vec, F32), jax.Sha...]
where the time goes in v4:
time: 146 us
  Pallas kernels  139 us (95%)
  local copies, waits for them, and re-layouts  4.11 us (3%)
  other arithmetic  1.92 us (1%)
    pallas_call x1, Pallas kernels, local(): pl.pallas_call(kernel, out_shape=(jax.ShapeDtypeStruct(vec, F32), jax.Sha...  139 us
    unnamed x4, local copies, waits for them, and re-layouts  4.11 us

profile of v4, /device:TPU:1, one launch (start us, length us, event | category | flops | bytes accessed | tf_op | source)
XLA Modules:
  0.0 146.1 jit_solution(7042348965821316924)
XLA Ops:
  0.6 0.7 compare_select_fusion.1
  1.3 0.7 select_reduce_fusion
  2.0 0.5 compare_select_fusion.links
  2.5 139.5 %gmres.1 = (f32[2,2048,128]{2,1,0:T(8,128)}, f32[2048,128]{1,0:T(8,128)}) custom-call(s32[8,16]{1,0:T(8,128)} %bitcast.14, s32[1,32]{1,0:T(1,128)} %bitcast.15, s32[32]{0:T(128)} %csrc.1, s32[48]{0:T(128)} %compare_select_fusion.links, f32[1,2]{1,0:T(1,128)} %pulse.1, f32[2,2048,128]{2,1,0:T(8,128)} %bitcast.10, f32[2,2048,128]{2,1,0:T(8,128)} %bitcast.11, ...), custom_call_target="tpu_custom_call" | custom-call | tf_op jit(solution)/shard_map/gmres/pallas_call | solution.py:620
  142.0 0.0 copy-start
  142.0 3.1 %copy.13 = f32[1,2,2048,128]{3,2,1,0:T(8,128)} copy(f32[1,2,2048,128]{3,2,1,0:T(8,128)} %bitcast.9) | data formatting | bytes 4194304
  145.2 0.0 copy-done
  145.2 1.0 copy.14
Async XLA Ops:
  142.0 3.1 %copy-start = (f32[2048,128]{1,0:T(8,128)S(1)}, f32[2048,128]{1,0:T(8,128)}, u32[]{:S(2)}) copy-start(f32[2048,128]{1,0:T(8,128)} %get-tuple-element.5) | copy-start | bytes 3145732
